TPU v7x, 512 devices: a whole 4x8x8 slice. The times are simulated.
512 devices in a mesh: context: 64 (over y, z), channel: 8 (over x, core).
Axes of the slice: x: 4, y: 8, z: 8, core: 2. Of those that a mesh axis runs over, the one named last changes fastest.
Arguments:
- inputs: bfloat16 [512, 32768], P('channel', 'context'), may hold values from -6 to 6
- grad_out: bfloat16 [512, 32768], P('channel', 'context'), may hold values from -36 to 36
- decay_rates: float32 [64, 16], replicated, as said below
- residues: float32 [64, 16], replicated, may hold values from -1.5 to 1.5
Outputs:
- grad_in: bfloat16 [512, 32768], P('channel', 'context')
- grad_residue: float32 [64, 16], replicated
- grad_log_rate: float32 [64, 16], replicated
Inputs may be any that keep to these rules, and one draw needn't show every extreme that they name: `decay_rates`: every rate lies between 0.3 / 32768 and 1 / 15.
All inputs are finite; a program needn't handle non-finite values.
Results may differ from a plain program's by a relative error of at most 0.001.
Values may be sent and summed in bfloat16 or wider, within the bound.
No kernel may reach another device: no remote copies, remote signals or barrier semaphores. Data moves between devices by JAX's collectives and lax.ppermute only.
A program may use at most 64 MiB of HBM per device.

v0:
```python
import math

import jax
import jax.numpy as jnp
from jax import lax
from jax.sharding import PartitionSpec as P

precise_setting = lax.Precision.HIGHEST


def forward_combine(earlier, later):
    decay_one, cross_one, state_one, slope_one = earlier
    decay_two, cross_two, state_two, second_slope = later
    return (
        decay_two * decay_one,
        decay_two * cross_one + cross_two * decay_one,
        decay_two * state_one + state_two,
        decay_two * slope_one + cross_two * state_one + second_slope,
    )


def backward_combine(earlier, later):
    decay_far, total_far = earlier
    decay_near, total_near = later
    return (decay_far * decay_near, total_near + decay_near * total_far)


def within_blocks(x_rows, g_rows, decay_rates, block_len):
    chan_count, pole_count = decay_rates.shape
    quarter = pole_count // 4
    offset = jnp.arange(block_len, dtype=jnp.float32)
    centre = float(block_len // 2)
    upper_ones = (offset[:, None] <= offset[None, :]).astype(jnp.float32)
    grouped = decay_rates.reshape(chan_count, 4, quarter).transpose(1, 0, 2)

    def one_group(rate_part):
        rate_col = rate_part[:, :, None]
        x_scaled = x_rows[:, None, :, :] * jnp.exp(-rate_col * (centre - offset))[:, :, None, :]
        g_scaled = g_rows[:, None, :, :] * jnp.exp(-rate_col * (offset - centre))[:, :, None, :]
        stacked = jnp.stack([x_scaled, x_scaled * offset], axis=2)
        running = jnp.einsum("nqsbv,vu->nqsbu", stacked, upper_ones, precision=precise_setting)
        first_part = jnp.sum(g_scaled * running[:, :, 0], axis=(2, 3))
        second_part = jnp.sum(
            g_scaled * (offset * running[:, :, 0] - running[:, :, 1]), axis=(2, 3)
        )
        return (first_part, second_part)

    first_all, second_all = lax.map(one_group, grouped)
    return (
        first_all.transpose(1, 0, 2).reshape(chan_count, pole_count),
        second_all.transpose(1, 0, 2).reshape(chan_count, pole_count),
    )


def prepare(inputs, grad_out, decay_rates, block_len):
    chan_count, length = inputs.shape
    blocks = length // block_len
    x_rows = inputs.astype(jnp.float32).reshape(chan_count, blocks, block_len)
    g_rows = grad_out.astype(jnp.float32).reshape(chan_count, blocks, block_len)
    offset = jnp.arange(block_len, dtype=jnp.float32)
    tail_pos = block_len - 1.0 - offset
    rate_col = decay_rates[:, :, None]
    tail_pow = jnp.exp(-rate_col * tail_pos)
    next_pow = jnp.exp(-rate_col * (offset + 1.0))
    x_weights = jnp.stack([tail_pow, tail_pos * tail_pow], axis=2)
    g_weights = jnp.stack(
        [next_pow, (offset + 1.0) * next_pow, jnp.exp(-rate_col * offset)], axis=2
    )
    x_ends = jnp.einsum("nbj,nksj->nksb", x_rows, x_weights, precision=precise_setting)
    g_ends = jnp.einsum("nbj,nksj->nksb", g_rows, g_weights, precision=precise_setting)
    block_decay = jnp.broadcast_to(
        jnp.exp(-decay_rates * block_len)[:, :, None], x_ends[:, :, 0].shape
    )
    forward = lax.associative_scan(
        forward_combine,
        (block_decay, block_len * block_decay, x_ends[:, :, 0], x_ends[:, :, 1]),
        axis=2,
    )
    backward = lax.associative_scan(
        backward_combine, (block_decay, g_ends[:, :, 2]), axis=2, reverse=True
    )
    first_in, second_in = within_blocks(x_rows, g_rows, decay_rates, block_len)
    return (g_rows, forward, backward, g_ends, first_in, second_in)


def complete(prepared, start_state, start_slope, end_adjoint, decay_rates, residues, block_len):
    g_rows, forward, backward, g_ends, first_in, second_in = prepared
    chan_count, blocks, _ = g_rows.shape
    unit_col = jnp.ones(decay_rates.shape + (1,), jnp.float32)
    zero_col = jnp.zeros_like(unit_col)
    lead_decay = jnp.concatenate([unit_col, forward[0][:, :, :-1]], axis=2)
    lead_cross = jnp.concatenate([zero_col, forward[1][:, :, :-1]], axis=2)
    lead_state = jnp.concatenate([zero_col, forward[2][:, :, :-1]], axis=2)
    lead_slope = jnp.concatenate([zero_col, forward[3][:, :, :-1]], axis=2)
    enter_state = lead_decay * start_state[:, :, None] + lead_state
    enter_slope = (
        lead_decay * start_slope[:, :, None] + lead_cross * start_state[:, :, None] + lead_slope
    )
    first_sum = first_in + jnp.sum(enter_state * g_ends[:, :, 0], axis=2)
    second_sum = second_in + jnp.sum(
        enter_slope * g_ends[:, :, 0] + enter_state * g_ends[:, :, 1], axis=2
    )
    decay_step = jnp.exp(-decay_rates)
    gain_pole = jnp.sqrt(-jnp.expm1(-2.0 * decay_rates))
    residue_gradient = gain_pole * first_sum
    log_grad = (
        residues
        * decay_rates
        * (decay_step * decay_step / gain_pole * first_sum - gain_pole * second_sum)
    )
    weighted = residues * gain_pole
    trail_decay = jnp.concatenate([backward[0][:, :, 1:], unit_col], axis=2)
    trail_total = jnp.concatenate([backward[1][:, :, 1:], zero_col], axis=2)
    incoming = (trail_total + trail_decay * end_adjoint[:, :, None]) * weighted[:, :, None]
    offset = jnp.arange(block_len, dtype=jnp.float32)
    centre = float(block_len // 2)
    rate_col = decay_rates[:, :, None]
    carried = jnp.einsum(
        "nkb,nkj->nbj",
        incoming,
        jnp.exp(-rate_col * (block_len - offset)),
        precision=precise_setting,
    )
    row_multiplier = weighted[:, :, None] * jnp.exp(-rate_col * (offset - centre))
    column_multiplier = jnp.exp(rate_col * (offset - centre))
    lower_mask = offset[:, None] >= offset[None, :]
    toeplitz = jnp.where(
        lower_mask[None],
        jnp.einsum("acr,acq->arq", row_multiplier, column_multiplier, precision=precise_setting),
        0.0,
    )
    local_part = jnp.einsum("nbu,nuv->nbv", g_rows, toeplitz, precision=precise_setting)
    grad_in = (local_part + carried).reshape(chan_count, blocks * block_len).astype(jnp.bfloat16)
    return (grad_in, residue_gradient, log_grad)


def body(inputs, grad_out, decay_rates, residues):
    chan_count, token_count = inputs.shape
    context_size = lax.axis_size("context")
    seq_total = token_count * context_size
    group_size = lax.axis_size("channel")
    pole_count = decay_rates.shape[1]
    zero_pair = jnp.zeros_like(decay_rates)
    share = chan_count // context_size
    moved_inputs, moved_grads = (
        lax.all_to_all(inputs, "context", split_axis=0, concat_axis=1, tiled=True),
        lax.all_to_all(grad_out, "context", split_axis=0, concat_axis=1, tiled=True),
    )
    first_row = lax.axis_index("context") * share
    my_rates = lax.dynamic_slice_in_dim(decay_rates, first_row, share, 0)
    my_residues = lax.dynamic_slice_in_dim(residues, first_row, share, 0)
    block_len = math.gcd(128, seq_total)
    prepared = prepare(moved_inputs, moved_grads, my_rates, block_len)
    zero_state = jnp.zeros((share, pole_count), jnp.float32)
    grad_part, res_part, log_part = complete(
        prepared, zero_state, zero_state, zero_state, my_rates, my_residues, block_len
    )
    grad_in = lax.all_to_all(grad_part, "context", split_axis=1, concat_axis=0, tiled=True)
    res_local = lax.dynamic_update_slice_in_dim(zero_pair, res_part, first_row, 0)
    log_local = lax.dynamic_update_slice_in_dim(zero_pair, log_part, first_row, 0)
    res_total, log_total = lax.psum((res_local, log_local), ("context", "channel"))
    norm_scale = 1.0 / math.sqrt(seq_total * group_size)
    return (grad_in, res_total * norm_scale, log_total * norm_scale)


def solution(mesh):
    return jax.shard_map(
        body,
        mesh=mesh,
        in_specs=(P("channel", "context"), P("channel", "context"), P(), P()),
        out_specs=(P("channel", "context"), P(), P()),
        check_vma=False,
    )
```

profile of v0, /device:TPU:1, one launch (start us, length us, event | category | flops | bytes accessed | tf_op | source)
XLA Modules:
  0.0 199.6 jit_solution(9558295038052606538)
XLA Ops:
  1.1 1.5 reduce.24
  2.6 0.6 reshape.1135
  3.3 17.3 %all-to-all-start.2 = ((bf16[64,2,256]{2,1,0:T(2,128)(2,1)}), bf16[64,2,256]{2,1,0:T(2,128)(2,1)S(1)}, u32[]{:S(2)}, u32[]{:S(2)}) async-start(bf16[64,2,256]{2,1,0:T(2,128)(2,1)} %reshape.1135), calls=%async_computation.2 | async-start | bytes 131072 | tf_op jit(solution)/shard_map/all_to_all | solution.py:146
  20.6 0.7 copy-done.1
  22.4 0.7 reduce.25
  23.1 0.6 reshape.1131
  23.7 7.9 %all-to-all-done.2 = bf16[64,2,256]{2,1,0:T(2,128)(2,1)S(1)} async-done(((bf16[64,2,256]{2,1,0:T(2,128)(2,1)}), bf16[64,2,256]{2,1,0:T(2,128)(2,1)S(1)}, u32[]{:S(2)}, u32[]{:S(2)}) %all-to-all-start.2) | async-done | bytes 65568 | tf_op jit(solution)/shard_map/all_to_all | solution.py:146
  31.7 4.8 %all-to-all-start = ((bf16[64,2,256]{2,1,0:T(2,128)(2,1)}), bf16[64,2,256]{2,1,0:T(2,128)(2,1)S(1)}, u32[]{:S(2)}, u32[]{:S(2)}) async-start(bf16[64,2,256]{2,1,0:T(2,128)(2,1)} %reshape.1131), calls=%async_computation | async-start | bytes 131072 | tf_op jit(solution)/shard_map/all_to_all | solution.py:147
  43.7 3.7 %all-to-all-done = bf16[64,2,256]{2,1,0:T(2,128)(2,1)S(1)} async-done(((bf16[64,2,256]{2,1,0:T(2,128)(2,1)}), bf16[64,2,256]{2,1,0:T(2,128)(2,1)S(1)}, u32[]{:S(2)}, u32[]{:S(2)}) %all-to-all-start) | async-done | bytes 65568 | tf_op jit(solution)/shard_map/all_to_all | solution.py:147
  68.6 6.0 %while.16 = (s32[]{:T(128)}, f32[4,1,4]{2,1,0:T(1,128)S(1)}, f32[4,1,4]{2,1,0:T(1,128)S(1)}, f32[1,32768]{1,0:T(1,128)S(1)}, f32[4,1,4]{2,1,0:T(1,128)S(1)}, /*index=5*/f32[1,32768]{1,0:T(1,128)S(1)}, s32[]{:T(128)}) while((s32[]{:T(128)}, f32[4,1,4]{2,1,0:T(1,128)S(1)}, f32[4,1,4]{2,1,0:T(1,128)S(1)}, ...), condition=%wide.region_3.4_spmd.clone.clone, body=%wide.region_0.3_spmd.clone.clone.sunk | while | flops 404129024 | bytes 4468909 | solution.py:48
  69.0 1.0 convolution_bitcast_fusion.5
  70.4 1.0 convolution_bitcast_fusion.5
  71.9 1.0 convolution_bitcast_fusion.5
  73.3 1.0 convolution_bitcast_fusion.5
  75.1 0.7 reduce.22
  75.8 0.7 reduce.21
  80.1 96.9 %all-reduce.102 = (f32[64,16]{0,1:T(8,128)S(1)}, f32[64,16]{0,1:T(8,128)S(1)}) all-reduce(f32[64,16]{0,1:T(8,128)S(1)} %dynamic_update_slice.19, f32[64,16]{0,1:T(8,128)S(1)} %dynamic_update_slice.20), channel_id=1, replica_groups=mesh['context'=64,'channel'=8] {'context','channel'}, use_global_device_ids=true, to_apply=%region_5.6 | all-reduce | flops 2048 | bytes 16384 | tf_op jit(solution)/shard_map/psum | solution.py:161
  177.0 0.6 broadcast_multiply_fusion.3
  178.8 1.0 reduce.26
  179.8 0.6 reshape.1133
  180.5 7.2 %all-to-all-start.1 = ((bf16[64,2,256]{2,1,0:T(2,128)(2,1)}), bf16[64,2,256]{2,1,0:T(2,128)(2,1)S(1)}, u32[]{:S(2)}, u32[]{:S(2)}) async-start(bf16[64,2,256]{2,1,0:T(2,128)(2,1)} %reshape.1133), calls=%async_computation.1 | async-start | bytes 131072 | tf_op jit(solution)/shard_map/all_to_all | solution.py:158
  187.7 0.6 broadcast_multiply_fusion.2
  188.3 10.5 %all-to-all-done.1 = bf16[64,2,256]{2,1,0:T(2,128)(2,1)S(1)} async-done(((bf16[64,2,256]{2,1,0:T(2,128)(2,1)}), bf16[64,2,256]{2,1,0:T(2,128)(2,1)S(1)}, u32[]{:S(2)}, u32[]{:S(2)}) %all-to-all-start.1) | async-done | bytes 65568 | tf_op jit(solution)/shard_map/all_to_all | solution.py:158
  198.9 0.6 copy.204
  (375 shorter events, 36.1 us)
Async XLA Ops:
  3.3 17.3 %copy-start.2 = (f32[64,16]{0,1:T(8,128)S(1)}, f32[64,16]{0,1:T(8,128)}, u32[]{:S(2)}) copy-start(f32[64,16]{0,1:T(8,128)} %param.9) | copy-start | bytes 12292
  3.3 28.4 %all-to-all-start.2 = ((bf16[64,2,256]{2,1,0:T(2,128)(2,1)}), bf16[64,2,256]{2,1,0:T(2,128)(2,1)S(1)}, u32[]{:S(2)}, u32[]{:S(2)}) async-start(bf16[64,2,256]{2,1,0:T(2,128)(2,1)} %reshape.1135), calls=%async_computation.2 | async-start | bytes 131072 | tf_op jit(solution)/shard_map/all_to_all | solution.py:146
  20.6 0.7 copy-start.1
  21.6 0.8 copy-start
  31.7 15.7 %all-to-all-start = ((bf16[64,2,256]{2,1,0:T(2,128)(2,1)}), bf16[64,2,256]{2,1,0:T(2,128)(2,1)S(1)}, u32[]{:S(2)}, u32[]{:S(2)}) async-start(bf16[64,2,256]{2,1,0:T(2,128)(2,1)} %reshape.1131), calls=%async_computation | async-start | bytes 131072 | tf_op jit(solution)/shard_map/all_to_all | solution.py:147
  180.5 18.4 %all-to-all-start.1 = ((bf16[64,2,256]{2,1,0:T(2,128)(2,1)}), bf16[64,2,256]{2,1,0:T(2,128)(2,1)S(1)}, u32[]{:S(2)}, u32[]{:S(2)}) async-start(bf16[64,2,256]{2,1,0:T(2,128)(2,1)} %reshape.1133), calls=%async_computation.1 | async-start | bytes 131072 | tf_op jit(solution)/shard_map/all_to_all | solution.py:158
where the time goes:
time: 200 us
  blocking collectives  96.9 us (48%)
  local copies, waits for them, and re-layouts  29.6 us (15%)
  starting transfers between devices  29.3 us (15%)
  waiting for transfers between devices  22.1 us (11%)
  other arithmetic  14.1 us (7%)
  matrix products  5.37 us (3%)
    psum x1, blocking collectives, body(): lax.psum((res_local, log_local), ('context', 'channel'))  96.9 us
    all_to_all x1, starting transfers between devices, body(): lax.all_to_all(inputs, 'context', split_axis=0, concat_axis=1, tiled=True)  17.3 us
    all_to_all x1, waiting for transfers between devices, body(): lax.all_to_all(grad_part, 'context', split_axis=1, concat_axis=0, tiled=T...  10.5 us
    all_to_all x1, waiting for transfers between devices, body(): lax.all_to_all(inputs, 'context', split_axis=0, concat_axis=1, tiled=True)  7.95 us
    all_to_all x1, starting transfers between devices, body(): lax.all_to_all(grad_part, 'context', split_axis=1, concat_axis=0, tiled=T...  7.24 us
    unnamed x26, local copies, waits for them, and re-layouts  6.29 us
    slice x43, local copies, waits for them, and re-layouts, prepare(): lax.associative_scan(forward_combine, (block_decay, block_len * block_dec...  6.06 us
    slice x46, local copies, waits for them, and re-layouts, prepare(): lax.associative_scan(backward_combine, (block_decay, g_ends[:, :, 2]), ax...  5.62 us
  transfers between devices with their start and end apart: 3, of which 3 were waited for; matrix products, arithmetic and copies ran while one was open for 5% of the time, Pallas kernels for 0%

commit v1 on v0

v1 whole, which is shorter than its diff:
```python
import functools
import math

import jax
import jax.numpy as jnp
from jax import lax
from jax.experimental import pallas as pl
from jax.experimental.pallas import tpu as pltpu
from jax.sharding import PartitionSpec as P

LANES = 128
SUBLANES = 8
CHANNELS = 64
POLES = 16
STEP = 32
HALF = SUBLANES * STEP
CHUNK = 2 * HALF
ROWS = 8
GROUP = 8


def low_half(shape):
    return lax.broadcasted_iota(jnp.int32, shape, len(shape) - 1) < CHANNELS


def double(rows):
    return jnp.concatenate([rows, rows], axis=1)


def pack(ref):
    even = ref[pl.ds(0, SUBLANES, stride=2), :]
    odd = ref[pl.ds(1, SUBLANES, stride=2), :]
    return jnp.where(low_half(even.shape), even, odd)


def transposed(block):
    stacked = jnp.concatenate([block[:, :HALF], block[:, HALF:]], axis=0)
    return stacked.astype(jnp.float32).T


def pre_kernel(x_ref, g_ref, rate_ref, msg_ref, ain_ref, gt_ref, xt_ref, rate2_ref, rows_ref, blk_ref):
    gt_ref[...] = transposed(g_ref[...])
    xt_ref[...] = transposed(x_ref[...])
    rate2_ref[...] = double(rate_ref[...])
    full = (SUBLANES, LANES)
    low = low_half(full)
    block = lax.broadcasted_iota(jnp.int32, full, 0)
    after = (SUBLANES - 1 - block).astype(jnp.float32)
    after_all = jnp.where(low, after + SUBLANES, after)
    zero = jnp.zeros(full, jnp.float32)
    for first in range(0, POLES, 8):
        poles = range(first, first + 8)
        decay = [jnp.broadcast_to(jnp.exp(-rate2_ref[pl.ds(k, 1), :]), full) for k in poles]
        total = [zero] * 8
        slope = [zero] * 8
        value = [zero] * 8
        tilt = [zero] * 8
        for j in reversed(range(STEP)):
            g = gt_ref[pl.ds(j, SUBLANES, stride=STEP), :]
            x = xt_ref[pl.ds(j, SUBLANES, stride=STEP), :]
            for i in range(8):
                slope[i] = decay[i] * (slope[i] + total[i])
                total[i] = decay[i] * total[i] + g
                value[i] = value[i] + x * total[i]
                tilt[i] = tilt[i] + x * slope[i]
        for i, k in enumerate(poles):
            blk_ref[0, k] = total[i]
            blk_ref[1, k] = slope[i]
            blk_ref[2, k] = value[i]
            blk_ref[3, k] = tilt[i]
        state = [zero] * 8
        lean = [zero] * 8
        for j in range(STEP):
            x = xt_ref[pl.ds(j, SUBLANES, stride=STEP), :]
            for i in range(8):
                state[i] = decay[i] * (state[i] + x)
                lean[i] = decay[i] * lean[i] + state[i]
        for i, k in enumerate(poles):
            blk_ref[4, k] = state[i]
            blk_ref[5, k] = lean[i]
    for k in range(POLES):
        rate = rate2_ref[pl.ds(k, 1), :]
        total, slope = blk_ref[0, k], blk_ref[1, k]
        state, lean = blk_ref[4, k], blk_ref[5, k]
        for shift in (1, 2, 4):
            far = jnp.where(block < SUBLANES - shift, jnp.exp(-(STEP * shift) * rate), 0.0)
            moved = pltpu.roll(total, SUBLANES - shift, 0)
            turned = pltpu.roll(slope, SUBLANES - shift, 0)
            slope = slope + far * (turned + float(STEP * shift) * moved)
            total = total + far * moved
        rows_ref[0, pl.ds(k, 1), :] = total[0:1]
        rows_ref[1, pl.ds(k, 1), :] = slope[0:1]
        inside = block < SUBLANES - 1
        moved = jnp.where(inside, pltpu.roll(total, SUBLANES - 1, 0), 0.0)
        turned = jnp.where(inside, pltpu.roll(slope, SUBLANES - 1, 0), 0.0)
        late = jnp.where(low, pltpu.roll(jnp.broadcast_to(total[0:1], full), CHANNELS, 1), 0.0)
        late_slope = jnp.where(low, pltpu.roll(jnp.broadcast_to(slope[0:1], full), CHANNELS, 1), 0.0)
        reach = jnp.exp(-(float(STEP) * after) * rate)
        coming = moved + reach * late
        coming_slope = turned + reach * (late_slope + (float(STEP) * after) * late)
        ain_ref[k] = coming
        value = blk_ref[2, k] + state * coming
        tilt = blk_ref[3, k] + lean * coming + state * coming_slope
        away = float(STEP) * after_all
        weight = jnp.exp(-away * rate)
        rows_ref[2, pl.ds(k, 1), :] = jnp.sum(weight * state, axis=0, keepdims=True)
        rows_ref[3, pl.ds(k, 1), :] = jnp.sum(weight * (lean + away * state), axis=0, keepdims=True)
        rows_ref[4, pl.ds(k, 1), :] = jnp.sum(value, axis=0, keepdims=True)
        rows_ref[5, pl.ds(k, 1), :] = jnp.sum(tilt, axis=0, keepdims=True)
    rates = rate2_ref[...]
    low_rows = low_half(rates.shape)
    jump = jnp.where(low_rows, 1.0, jnp.exp(-float(HALF) * rates))
    length = jnp.where(low_rows, 0.0, float(HALF))
    rows_ref[1] = jump * (rows_ref[1] + length * rows_ref[0])
    rows_ref[0] = jump * rows_ref[0]
    for q in range(6):
        both = rows_ref[q] + pltpu.roll(rows_ref[q], CHANNELS, 1)
        rows_ref[q] = both
        packed = pack(rows_ref.at[q])
        for d in range(ROWS):
            msg_ref[d, pl.ds(q * SUBLANES, SUBLANES), :] = packed


def combine(recv_ref, rate, span):
    part = lambda d, q: recv_ref[d, pl.ds(q * SUBLANES, SUBLANES), :]
    decay = jnp.exp(-span * rate)
    coming = jnp.zeros_like(rate)
    coming_slope = jnp.zeros_like(rate)
    value = part(ROWS - 1, 4)
    tilt = part(ROWS - 1, 5)
    arriving = [coming] * ROWS
    for d in reversed(range(ROWS - 1)):
        coming_slope = part(d + 1, 1) + decay * (coming_slope + span * coming)
        coming = part(d + 1, 0) + decay * coming
        arriving[d] = coming
        value = value + part(d, 4) + part(d, 2) * coming
        tilt = tilt + part(d, 5) + part(d, 3) * coming + part(d, 2) * coming_slope
    slope = part(0, 1) + decay * (coming_slope + span * coming)
    total = part(0, 0) + decay * coming
    state = part(0, 2)
    lean = part(0, 3)
    for d in range(1, ROWS):
        lean = part(d, 3) + decay * (lean + span * state)
        state = part(d, 2) + decay * state
    return total, slope, state, lean, value, tilt, arriving


def pick(at, choices):
    out = choices[0]
    for d in range(1, ROWS):
        out = jnp.where(at == d, choices[d], out)
    return out


def row_kernel(at_ref, recv_ref, rate_ref, msg_ref, arrive_ref, rate2_ref):
    rate2_ref[...] = double(rate_ref[...])
    rate = pack(rate2_ref)
    *sums, arriving = combine(recv_ref, rate, float(CHUNK))
    for q, packed in enumerate(sums):
        for d in range(ROWS):
            msg_ref[d, pl.ds(q * SUBLANES, SUBLANES), :] = packed
    arrive_ref[...] = pick(at_ref[0], arriving)


def column_kernel(at_ref, recv_ref, rate_ref, arrive_ref, msg_ref, state_ref, rate2_ref):
    rate2_ref[...] = double(rate_ref[...])
    rate = pack(rate2_ref)
    sums = combine(recv_ref, rate, float(CHUNK * ROWS))
    for q in range(2):
        for d in range(GROUP):
            msg_ref[d, pl.ds(q * SUBLANES, SUBLANES), :] = sums[4 + q]
    after = float(CHUNK) * (ROWS - 1 - at_ref[0]).astype(jnp.float32)
    state_ref[...] = arrive_ref[...] + jnp.exp(-after * rate) * pick(at_ref[1], sums[6])


def post_kernel(g_ref, rate_ref, weight_ref, ain_ref, state_ref, out_ref, gt_ref, yt_ref, rate2_ref, weight2_ref):
    gt_ref[...] = transposed(g_ref[...])
    rate2_ref[...] = double(rate_ref[...])
    weight2_ref[...] = double(weight_ref[...])
    full = (SUBLANES, LANES)
    low = low_half(full)
    low_row = low_half((1, LANES))
    after = (SUBLANES - 1 - lax.broadcasted_iota(jnp.int32, full, 0)).astype(jnp.float32)
    away = float(STEP) * jnp.where(low, after + SUBLANES, after)
    for first in range(0, POLES, 8):
        poles = range(first, first + 8)
        decay = [jnp.broadcast_to(jnp.exp(-rate2_ref[pl.ds(k, 1), :]), full) for k in poles]
        weight = [jnp.broadcast_to(weight2_ref[pl.ds(k, 1), :], full) for k in poles]
        total = []
        for k in poles:
            row = state_ref[pl.ds(k // 2, 1), :]
            other = pltpu.roll(row, CHANNELS, 1)
            both = jnp.where(low_row, row, other) if k % 2 == 0 else jnp.where(low_row, other, row)
            total.append(ain_ref[k] + jnp.exp(-away * rate2_ref[pl.ds(k, 1), :]) * both)
        for j in reversed(range(STEP)):
            at = pl.ds(j, SUBLANES, stride=STEP)
            g = gt_ref[at, :]
            for i in range(8):
                total[i] = decay[i] * total[i] + g
            terms = [weight[i] * total[i] for i in range(8)]
            while len(terms) > 1:
                terms = [terms[i] + terms[i + 1] for i in range(0, len(terms), 2)]
            yt_ref[at, :] = terms[0] if first == 0 else yt_ref[at, :] + terms[0]
    stacked = yt_ref[...].T
    out_ref[:, :HALF] = stacked[:CHANNELS].astype(jnp.bfloat16)
    out_ref[:, HALF:] = stacked[CHANNELS:].astype(jnp.bfloat16)


def final_kernel(recv_ref, one_ref, two_ref, three_ref, res_ref, log_ref):
    value = recv_ref[0, pl.ds(0, SUBLANES), :]
    tilt = recv_ref[0, pl.ds(SUBLANES, SUBLANES), :]
    for d in range(1, GROUP):
        value = value + recv_ref[d, pl.ds(0, SUBLANES), :]
        tilt = tilt + recv_ref[d, pl.ds(SUBLANES, SUBLANES), :]
    for k in range(POLES):
        lanes = slice(0, CHANNELS) if k % 2 == 0 else slice(CHANNELS, LANES)
        first = value[k // 2 : k // 2 + 1, lanes]
        second = tilt[k // 2 : k // 2 + 1, lanes]
        at = pl.ds(k, 1)
        res_ref[at, :] = one_ref[at, :] * first
        log_ref[at, :] = two_ref[at, :] * first - three_ref[at, :] * second


def vmem(count):
    return [pl.BlockSpec(memory_space=pltpu.VMEM)] * count


def f32(*shape):
    return jax.ShapeDtypeStruct(shape, jnp.float32)


def scratch(*shape):
    return pltpu.VMEM(shape, jnp.float32)


def body(inputs, grad_out, decay_rates, residues):
    rate = decay_rates.T
    residue = residues.T
    place = lax.axis_index("context")
    at = jnp.stack([place % ROWS, place // ROWS]).astype(jnp.int32)
    rows = [[y * ROWS + z for z in range(ROWS)] for y in range(ROWS)]
    columns = [[y * ROWS + z for y in range(ROWS)] for z in range(ROWS)]
    smem = [pl.BlockSpec(memory_space=pltpu.SMEM)]

    message, coming = pl.pallas_call(
        pre_kernel,
        out_shape=(f32(ROWS, 6 * SUBLANES, LANES), f32(POLES, SUBLANES, LANES)),
        in_specs=vmem(3),
        out_specs=tuple(vmem(2)),
        scratch_shapes=[
            scratch(HALF, LANES),
            scratch(HALF, LANES),
            scratch(POLES, LANES),
            scratch(6, POLES, LANES),
            scratch(6, POLES, SUBLANES, LANES),
        ],
        name="pre",
    )(inputs, grad_out, rate)
    received = lax.all_to_all(message, "context", 0, 0, axis_index_groups=rows, tiled=True)
    message, arrived = pl.pallas_call(
        row_kernel,
        out_shape=(f32(ROWS, 6 * SUBLANES, LANES), f32(SUBLANES, LANES)),
        in_specs=smem + vmem(2),
        out_specs=tuple(vmem(2)),
        scratch_shapes=[scratch(POLES, LANES)],
        name="row",
    )(at, received, rate)
    received = lax.all_to_all(message, "context", 0, 0, axis_index_groups=columns, tiled=True)
    message, state = pl.pallas_call(
        column_kernel,
        out_shape=(f32(GROUP, 2 * SUBLANES, LANES), f32(SUBLANES, LANES)),
        in_specs=smem + vmem(3),
        out_specs=tuple(vmem(2)),
        scratch_shapes=[scratch(POLES, LANES)],
        name="column",
    )(at, received, rate, arrived)
    received = lax.all_to_all(message, "channel", 0, 0, tiled=True)

    gain = jnp.sqrt(-jnp.expm1(-2.0 * rate))
    decay = jnp.exp(-rate)
    grad_in = pl.pallas_call(
        post_kernel,
        out_shape=jax.ShapeDtypeStruct((CHANNELS, CHUNK), jnp.bfloat16),
        in_specs=vmem(5),
        out_specs=vmem(1)[0],
        scratch_shapes=[scratch(HALF, LANES), scratch(HALF, LANES), scratch(POLES, LANES), scratch(POLES, LANES)],
        name="post",
    )(grad_out, rate, residue * gain, coming, state)
    norm = 1.0 / math.sqrt(CHUNK * ROWS * ROWS * GROUP)
    scaled = residue * rate * norm
    res_grad, log_grad = pl.pallas_call(
        final_kernel,
        out_shape=(f32(POLES, CHANNELS), f32(POLES, CHANNELS)),
        in_specs=vmem(4),
        out_specs=tuple(vmem(2)),
        name="final",
    )(received, gain * norm, scaled * (decay * decay / gain), scaled * gain)
    return (grad_in, res_grad.T, log_grad.T)


def solution(mesh):
    return jax.shard_map(
        body,
        mesh=mesh,
        in_specs=(P("channel", "context"), P("channel", "context"), P(), P()),
        out_specs=(P("channel", "context"), P(), P()),
        check_vma=False,
    )
```

time: 200 us -> 59.3 us (0.30)
  blocking collectives: 96.9 us -> 15.7 us
  local copies, waits for them, and re-layouts: 29.6 us -> 1.32 us
  other arithmetic: 14.1 us -> 1.22 us
  waiting for transfers between devices: 22.1 us -> 10.3 us
  Pallas kernels: 0 us -> 10.5 us
  starting transfers between devices: 29.3 us -> 19 us
  matrix products: 5.37 us -> 0 us
    psum x1 -> x0, blocking collectives: 96.9 us -> none  [body(): lax.psum((res_local, log_local), ('context', 'channel'))]
    all_to_all x0 -> x1, blocking collectives: none -> 15.7 us  [body(): lax.all_to_all(message, 'context', 0, 0, axis_index_groups=columns, tiled...]
    slice x95 -> x0, local copies, waits for them, and re-layouts: 13.7 us -> none  [the longest x43 6.06 us: prepare(): lax.associative_scan(forward_combine, (block_decay, block_len * block_dec...]
    all_to_all x3 -> x2, waiting for transfers between devices: 22.1 us -> 10.3 us  [the longest x1 8.41 us: body(): lax.all_to_all(message, 'context', 0, 0, axis_index_groups=rows, tiled=True)]
    pallas_call x0 -> x5, Pallas kernels: none -> 10.5 us  [the longest x1 3.19 us: body(): pl.pallas_call(pre_kernel, out_shape=(f32(ROWS, 6 * SUBLANES, LANES), f32...]
    all_to_all x3 -> x2, starting transfers between devices: 29.3 us -> 19 us  [the longest x1 10.9 us: body(): lax.all_to_all(message, 'context', 0, 0, axis_index_groups=rows, tiled=True)]
    pad x72 -> x0, local copies, waits for them, and re-layouts: 7.71 us -> none  [the longest x48 5.15 us: prepare(): lax.associative_scan(forward_combine, (block_decay, block_len * block_dec...]
    dot_general x9 -> x0, matrix products: 5.37 us -> none  [the longest x4 3.96 us: one_group(): jnp.einsum('nqsbv,vu->nqsbu', stacked, upper_ones, precision=precise_sett...]
  transfers between devices with their start and end apart: 3 -> 2, of which waited for: 3 -> 2; matrix products, arithmetic and copies ran while one was open for 5% -> 2% of each run, Pallas kernels for 0% -> 4%
where the time goes in v1:
time: 59.3 us; the launch traced here: 58.7 us
  starting transfers between devices  19 us (32%)
  blocking collectives  15.7 us (26%)
  Pallas kernels  10.5 us (18%)
  waiting for transfers between devices  10.3 us (17%)
  local copies, waits for them, and re-layouts  1.32 us (2%)
  other arithmetic  1.22 us (2%)
  between operations  0.64 us (1%)
    all_to_all x1, blocking collectives, body(): lax.all_to_all(message, 'context', 0, 0, axis_index_groups=columns, tiled...  15.7 us
    all_to_all x1, starting transfers between devices, body(): lax.all_to_all(message, 'context', 0, 0, axis_index_groups=rows, tiled=True)  10.9 us
    all_to_all x1, waiting for transfers between devices, body(): lax.all_to_all(message, 'context', 0, 0, axis_index_groups=rows, tiled=True)  8.41 us
    all_to_all x1, starting transfers between devices, body(): received = lax.all_to_all(message, 'channel', 0, 0, tiled=True)  8.19 us
    pallas_call x1, Pallas kernels, body(): pl.pallas_call(pre_kernel, out_shape=(f32(ROWS, 6 * SUBLANES, LANES), f32...  3.19 us
    pallas_call x1, Pallas kernels, body(): pl.pallas_call(post_kernel, out_shape=jax.ShapeDtypeStruct((CHANNELS, CHU...  2.32 us
    all_to_all x1, waiting for transfers between devices, body(): received = lax.all_to_all(message, 'channel', 0, 0, tiled=True)  1.88 us
    pallas_call x1, Pallas kernels, body(): pl.pallas_call(row_kernel, out_shape=(f32(ROWS, 6 * SUBLANES, LANES), f32...  1.73 us
  transfers between devices with their start and end apart: 2, of which 2 were waited for; matrix products, arithmetic and copies ran while one was open for 2% of the time, Pallas kernels for 4%

profile of v1, /device:TPU:1, one launch (start us, length us, event | category | flops | bytes accessed | tf_op | source)
XLA Modules:
  0.0 58.7 jit_solution(2004797007242461232)
XLA Ops:
  0.6 3.2 %pre.1 = (f32[8,48,128]{2,1,0:T(8,128)}, f32[16,8,128]{2,1,0:T(8,128)}) custom-call(bf16[64,512]{1,0:T(8,128)(2,1)} %x_ref.1, bf16[64,512]{1,0:T(8,128)(2,1)} %g_ref.3, f32[16,64]{1,0:T(8,128)} %bitcast.18), custom_call_target="tpu_custom_call" | custom-call | tf_op jit(solution)/shard_map/pre/pallas_call | solution.py:245
  3.8 10.9 %all-to-all-start = ((f32[8,48,128]{2,1,0:T(8,128)}), f32[8,48,128]{2,1,0:T(8,128)S(1)}, u32[]{:S(2)}, u32[]{:S(2)}) async-start(f32[8,48,128]{2,1,0:T(8,128)} %get-tuple-element.12), calls=%async_computation | async-start | bytes 393216 | tf_op jit(solution)/shard_map/all_to_all | solution.py:259
  14.7 0.6 pad_add_fusion.at_ref
  15.3 8.4 %all-to-all-done.recv_ref = f32[8,48,128]{2,1,0:T(8,128)S(1)} async-done(((f32[8,48,128]{2,1,0:T(8,128)}), f32[8,48,128]{2,1,0:T(8,128)S(1)}, u32[]{:S(2)}, u32[]{:S(2)}) %all-to-all-start) | async-done | bytes 196640 | tf_op jit(solution)/shard_map/all_to_all | solution.py:259
  23.7 0.0 copy-start
  23.7 0.7 %copy-done = f32[8,48,128]{2,1,0:T(8,128)} copy-done((f32[8,48,128]{2,1,0:T(8,128)}, f32[8,48,128]{2,1,0:T(8,128)S(1)}, u32[]{:S(2)}) %copy-start) | copy-done | bytes 196632
  24.4 1.7 %row.1 = (f32[8,48,128]{2,1,0:T(8,128)}, f32[8,128]{1,0:T(8,128)}) custom-call(s32[2]{0:T(128)} %pad_add_fusion.at_ref, f32[8,48,128]{2,1,0:T(8,128)} %copy-done, f32[16,64]{1,0:T(8,128)} %bitcast.19), custom_call_target="tpu_custom_call" | custom-call | tf_op jit(solution)/shard_map/row/pallas_call | solution.py:260
  26.1 15.7 %all_to_all.15.recv_ref = f32[8,48,128]{2,1,0:T(8,128)} all-to-all(f32[8,48,128]{2,1,0:T(8,128)} %get-tuple-element.13), channel_id=1, replica_groups={{0,64,128,192,256,320,384,448},{8,72,136,200,264,328,392,456},{16,80,14..., dimensions={0} | all-to-all | bytes 393216 | tf_op jit(solution)/shard_map/all_to_all | solution.py:268
  41.7 1.7 %column.1 = (f32[8,16,128]{2,1,0:T(8,128)}, f32[8,128]{1,0:T(8,128)}) custom-call(s32[2]{0:T(128)} %pad_add_fusion.at_ref, f32[8,48,128]{2,1,0:T(8,128)} %all_to_all.15.recv_ref, f32[16,64]{1,0:T(8,128)} %bitcast.20, f32[8,128]{1,0:T(8,128)} %get-tuple-element.14.arrive_ref), custom_call_target="tpu_custom_call" | custom-call | tf_op jit(solution)/shard_map/column/pallas_call | solution.py:269
  43.4 0.0 copy-start.2
  43.4 0.0 copy-start.3
  43.4 8.2 %all-to-all-start.2 = ((f32[8,16,128]{2,1,0:T(8,128)}), f32[8,16,128]{2,1,0:T(8,128)S(1)}, u32[]{:S(2)}, u32[]{:S(2)}) async-start(f32[8,16,128]{2,1,0:T(8,128)} %get-tuple-element.16), calls=%async_computation.2 | async-start | bytes 131072 | tf_op jit(solution)/shard_map/all_to_all | solution.py:277
  51.6 0.0 copy-done.2
  51.6 0.0 copy-done.3
  51.6 0.6 %fusion.1 = (f32[16,64]{1,0:T(8,128)}, f32[16,64]{1,0:T(8,128)}, f32[16,64]{1,0:T(8,128)}, f32[16,64]{1,0:T(8,128)}) fusion(f32[64,16]{0,1:T(8,128)S(1)} %copy-done.3, f32[64,16]{0,1:T(8,128)S(1)} %copy-done.2), kind=kLoop, calls=%fused_computation.5 | loop fusion | flops 11264 | bytes 24576 | tf_op jit(solution)/shard_map/mul | solution.py:297
  52.3 2.3 %post.1 = bf16[64,512]{1,0:T(8,128)(2,1)} custom-call(bf16[64,512]{1,0:T(8,128)(2,1)} %g_ref.3, f32[16,64]{1,0:T(8,128)} %bitcast.21, f32[16,64]{1,0:T(8,128)} %get-tuple-element.21.weight_ref, f32[16,8,128]{2,1,0:T(8,128)} %get-tuple-element.11.ain_ref, f32[8,128]{1,0:T(8,128)} %get-tuple-element.15.state_ref), custom_call_target="tpu_custom_call" | custom-call | tf_op jit(solution)/shard_map/post/pallas_call | solution.py:281
  54.6 1.9 %all-to-all-done.2.recv_ref = f32[8,16,128]{2,1,0:T(8,128)S(1)} async-done(((f32[8,16,128]{2,1,0:T(8,128)}), f32[8,16,128]{2,1,0:T(8,128)S(1)}, u32[]{:S(2)}, u32[]{:S(2)}) %all-to-all-start.2) | async-done | bytes 65568 | tf_op jit(solution)/shard_map/all_to_all | solution.py:277
  56.5 0.0 copy-start.1
  56.5 0.6 %copy-done.1 = f32[8,16,128]{2,1,0:T(8,128)} copy-done((f32[8,16,128]{2,1,0:T(8,128)}, f32[8,16,128]{2,1,0:T(8,128)S(1)}, u32[]{:S(2)}) %copy-start.1) | copy-done | bytes 65560
  57.1 1.6 %final.1 = (f32[16,64]{1,0:T(8,128)}, f32[16,64]{1,0:T(8,128)}) custom-call(f32[8,16,128]{2,1,0:T(8,128)} %copy-done.1, f32[16,64]{1,0:T(8,128)} %get-tuple-element.22.one_ref, f32[16,64]{1,0:T(8,128)} %get-tuple-element.20.two_ref, f32[16,64]{1,0:T(8,128)} %get-tuple-element.19.three_ref), custom_call_target="tpu_custom_call" | custom-call | tf_op jit(solution)/shard_map/final/pallas_call | solution.py:291
Async XLA Ops:
  3.8 19.8 %all-to-all-start = ((f32[8,48,128]{2,1,0:T(8,128)}), f32[8,48,128]{2,1,0:T(8,128)S(1)}, u32[]{:S(2)}, u32[]{:S(2)}) async-start(f32[8,48,128]{2,1,0:T(8,128)} %get-tuple-element.12), calls=%async_computation | async-start | bytes 393216 | tf_op jit(solution)/shard_map/all_to_all | solution.py:259
  23.7 0.7 %copy-start = (f32[8,48,128]{2,1,0:T(8,128)}, f32[8,48,128]{2,1,0:T(8,128)S(1)}, u32[]{:S(2)}) copy-start(f32[8,48,128]{2,1,0:T(8,128)S(1)} %all-to-all-done.recv_ref) | copy-start | bytes 589828
  43.4 8.2 %copy-start.2 = (f32[64,16]{0,1:T(8,128)S(1)}, f32[64,16]{0,1:T(8,128)}, u32[]{:S(2)}) copy-start(f32[64,16]{0,1:T(8,128)} %param.6) | copy-start | bytes 12292
  43.4 8.2 %copy-start.3 = (f32[64,16]{0,1:T(8,128)S(1)}, f32[64,16]{0,1:T(8,128)}, u32[]{:S(2)}) copy-start(f32[64,16]{0,1:T(8,128)} %param.7) | copy-start | bytes 12292
  43.4 13.0 %all-to-all-start.2 = ((f32[8,16,128]{2,1,0:T(8,128)}), f32[8,16,128]{2,1,0:T(8,128)S(1)}, u32[]{:S(2)}, u32[]{:S(2)}) async-start(f32[8,16,128]{2,1,0:T(8,128)} %get-tuple-element.16), calls=%async_computation.2 | async-start | bytes 131072 | tf_op jit(solution)/shard_map/all_to_all | solution.py:277
  56.5 0.6 %copy-start.1 = (f32[8,16,128]{2,1,0:T(8,128)}, f32[8,16,128]{2,1,0:T(8,128)S(1)}, u32[]{:S(2)}) copy-start(f32[8,16,128]{2,1,0:T(8,128)S(1)} %all-to-all-done.2.recv_ref) | copy-start | bytes 196612

commit v2 on v1

--- a/solution.py
+++ b/solution.py
@@ -17,6 +17,7 @@
 CHUNK = 2 * HALF
 ROWS = 8
 GROUP = 8
+GRANT = pltpu.CompilerParams(vmem_limit_bytes=8 << 20)
 
 
 def low_half(shape):
@@ -38,10 +39,20 @@
     return stacked.astype(jnp.float32).T
 
 
-def pre_kernel(x_ref, g_ref, rate_ref, msg_ref, ain_ref, gt_ref, xt_ref, rate2_ref, rows_ref, blk_ref):
+def pre_kernel(_, x_hbm, g_hbm, rate_hbm, msg_ref, ain_ref, gt_ref, packed_ref, x_ref, g_ref, rate_ref, xt_ref, rate2_ref, rows_ref, blk_ref, sems):
+    copies = [
+        pltpu.make_async_copy(source, target, sems.at[i])
+        for i, (source, target) in enumerate(((rate_hbm, rate_ref), (g_hbm, g_ref), (x_hbm, x_ref)))
+    ]
+    for copy in copies:
+        copy.start()
+    copies[0].wait()
+    rate2_ref[...] = double(rate_ref[...])
+    packed_ref[...] = pack(rate2_ref)
+    copies[1].wait()
     gt_ref[...] = transposed(g_ref[...])
+    copies[2].wait()
     xt_ref[...] = transposed(x_ref[...])
-    rate2_ref[...] = double(rate_ref[...])
     full = (SUBLANES, LANES)
     low = low_half(full)
     block = lax.broadcasted_iota(jnp.int32, full, 0)
@@ -152,29 +163,26 @@
     return out
 
 
-def row_kernel(at_ref, recv_ref, rate_ref, msg_ref, arrive_ref, rate2_ref):
-    rate2_ref[...] = double(rate_ref[...])
-    rate = pack(rate2_ref)
+def row_kernel(at_ref, recv_ref, rate_ref, msg_ref, arrive_ref):
+    rate = rate_ref[...]
     *sums, arriving = combine(recv_ref, rate, float(CHUNK))
     for q, packed in enumerate(sums):
         for d in range(ROWS):
             msg_ref[d, pl.ds(q * SUBLANES, SUBLANES), :] = packed
-    arrive_ref[...] = pick(at_ref[0], arriving)
-
-
-def column_kernel(at_ref, recv_ref, rate_ref, arrive_ref, msg_ref, state_ref, rate2_ref):
-    rate2_ref[...] = double(rate_ref[...])
-    rate = pack(rate2_ref)
+    arrive_ref[...] = pick(lax.rem(at_ref[0], ROWS), arriving)
+
+
+def column_kernel(at_ref, recv_ref, rate_ref, arrive_ref, msg_ref, state_ref):
+    rate = rate_ref[...]
     sums = combine(recv_ref, rate, float(CHUNK * ROWS))
     for q in range(2):
         for d in range(GROUP):
             msg_ref[d, pl.ds(q * SUBLANES, SUBLANES), :] = sums[4 + q]
-    after = float(CHUNK) * (ROWS - 1 - at_ref[0]).astype(jnp.float32)
-    state_ref[...] = arrive_ref[...] + jnp.exp(-after * rate) * pick(at_ref[1], sums[6])
-
-
-def post_kernel(g_ref, rate_ref, weight_ref, ain_ref, state_ref, out_ref, gt_ref, yt_ref, rate2_ref, weight2_ref):
-    gt_ref[...] = transposed(g_ref[...])
+    after = float(CHUNK) * (ROWS - 1 - lax.rem(at_ref[0], ROWS)).astype(jnp.float32)
+    state_ref[...] = arrive_ref[...] + jnp.exp(-after * rate) * pick(lax.div(at_ref[0], ROWS), sums[6])
+
+
+def post_kernel(gt_ref, rate_ref, weight_ref, ain_ref, state_ref, out_ref, yt_ref, rate2_ref, weight2_ref):
     rate2_ref[...] = double(rate_ref[...])
     weight2_ref[...] = double(weight_ref[...])
     full = (SUBLANES, LANES)
@@ -236,44 +244,47 @@
 def body(inputs, grad_out, decay_rates, residues):
     rate = decay_rates.T
     residue = residues.T
-    place = lax.axis_index("context")
-    at = jnp.stack([place % ROWS, place // ROWS]).astype(jnp.int32)
+    at = lax.axis_index("context").astype(jnp.int32).reshape(1)
     rows = [[y * ROWS + z for z in range(ROWS)] for y in range(ROWS)]
     columns = [[y * ROWS + z for y in range(ROWS)] for z in range(ROWS)]
     smem = [pl.BlockSpec(memory_space=pltpu.SMEM)]
 
-    message, coming = pl.pallas_call(
+    message, coming, turned, packed = pl.pallas_call(
         pre_kernel,
-        out_shape=(f32(ROWS, 6 * SUBLANES, LANES), f32(POLES, SUBLANES, LANES)),
-        in_specs=vmem(3),
-        out_specs=tuple(vmem(2)),
+        out_shape=(f32(ROWS, 6 * SUBLANES, LANES), f32(POLES, SUBLANES, LANES), f32(HALF, LANES), f32(SUBLANES, LANES)),
+        in_specs=smem + [pl.BlockSpec(memory_space=pltpu.HBM)] * 3,
+        out_specs=tuple(vmem(4)),
         scratch_shapes=[
-            scratch(HALF, LANES),
+            pltpu.VMEM((CHANNELS, CHUNK), jnp.bfloat16),
+            pltpu.VMEM((CHANNELS, CHUNK), jnp.bfloat16),
+            scratch(POLES, CHANNELS),
             scratch(HALF, LANES),
             scratch(POLES, LANES),
             scratch(6, POLES, LANES),
             scratch(6, POLES, SUBLANES, LANES),
+            pltpu.SemaphoreType.DMA((3,)),
         ],
+        compiler_params=GRANT,
         name="pre",
-    )(inputs, grad_out, rate)
+    )(at, *(pltpu.with_memory_space_constraint(v, pltpu.HBM) for v in (inputs, grad_out, rate)))
     received = lax.all_to_all(message, "context", 0, 0, axis_index_groups=rows, tiled=True)
     message, arrived = pl.pallas_call(
         row_kernel,
         out_shape=(f32(ROWS, 6 * SUBLANES, LANES), f32(SUBLANES, LANES)),
         in_specs=smem + vmem(2),
         out_specs=tuple(vmem(2)),
-        scratch_shapes=[scratch(POLES, LANES)],
+        compiler_params=GRANT,
         name="row",
-    )(at, received, rate)
+    )(at, received, packed)
     received = lax.all_to_all(message, "context", 0, 0, axis_index_groups=columns, tiled=True)
     message, state = pl.pallas_call(
         column_kernel,
         out_shape=(f32(GROUP, 2 * SUBLANES, LANES), f32(SUBLANES, LANES)),
         in_specs=smem + vmem(3),
         out_specs=tuple(vmem(2)),
-        scratch_shapes=[scratch(POLES, LANES)],
+        compiler_params=GRANT,
         name="column",
-    )(at, received, rate, arrived)
+    )(at, received, packed, arrived)
     received = lax.all_to_all(message, "channel", 0, 0, tiled=True)
 
     gain = jnp.sqrt(-jnp.expm1(-2.0 * rate))
@@ -283,9 +294,10 @@
         out_shape=jax.ShapeDtypeStruct((CHANNELS, CHUNK), jnp.bfloat16),
         in_specs=vmem(5),
         out_specs=vmem(1)[0],
-        scratch_shapes=[scratch(HALF, LANES), scratch(HALF, LANES), scratch(POLES, LANES), scratch(POLES, LANES)],
+        scratch_shapes=[scratch(HALF, LANES), scratch(POLES, LANES), scratch(POLES, LANES)],
+        compiler_params=GRANT,
         name="post",
-    )(grad_out, rate, residue * gain, coming, state)
+    )(turned, rate, residue * gain, coming, state)
     norm = 1.0 / math.sqrt(CHUNK * ROWS * ROWS * GROUP)
     scaled = residue * rate * norm
     res_grad, log_grad = pl.pallas_call(
@@ -293,6 +305,7 @@
         out_shape=(f32(POLES, CHANNELS), f32(POLES, CHANNELS)),
         in_specs=vmem(4),
         out_specs=tuple(vmem(2)),
+        compiler_params=GRANT,
         name="final",
     )(received, gain * norm, scaled * (decay * decay / gain), scaled * gain)
     return (grad_in, res_grad.T, log_grad.T)

time: 59.3 us -> 52.9 us (0.89)
  blocking collectives: 15.7 us -> 35 us
  starting transfers between devices: 19 us -> 8.19 us
  waiting for transfers between devices: 10.3 us -> 3.49 us
  Pallas kernels: 10.5 us -> 5.23 us
  local copies, waits for them, and re-layouts: 1.32 us -> 0.01 us
  other arithmetic: 1.22 us -> 0.03 us
    all_to_all x0 -> x1, blocking collectives: none -> 19.6 us  [body(): lax.all_to_all(message, 'context', 0, 0, axis_index_groups=rows, tiled=True)]
    all_to_all x1 -> x0, starting transfers between devices: 10.9 us -> none  [body(): lax.all_to_all(message, 'context', 0, 0, axis_index_groups=rows, tiled=True)]
    all_to_all x1 -> x0, waiting for transfers between devices: 8.41 us -> none  [body(): lax.all_to_all(message, 'context', 0, 0, axis_index_groups=rows, tiled=True)]
    pallas_call x1, Pallas kernels: 1.73 us -> 0.04 us  [body(): pl.pallas_call(row_kernel, out_shape=(f32(ROWS, 6 * SUBLANES, LANES), f32...]
    all_to_all x1, waiting for transfers between devices: 1.88 us -> 3.49 us  [body(): received = lax.all_to_all(message, 'channel', 0, 0, tiled=True)]
    unnamed x8 -> x4, local copies, waits for them, and re-layouts: 1.32 us -> 0.01 us
    pallas_call x1, Pallas kernels: 1.7 us -> 0.67 us  [body(): pl.pallas_call(column_kernel, out_shape=(f32(GROUP, 2 * SUBLANES, LANES),...]
    pallas_call x1, Pallas kernels: 2.32 us -> 1.32 us  [body(): pl.pallas_call(post_kernel, out_shape=jax.ShapeDtypeStruct((CHANNELS, CHU...]
  transfers between devices with their start and end apart: 2 -> 1, of which waited for: 2 -> 1; matrix products, arithmetic and copies ran while one was open for 2% -> 0% of each run, Pallas kernels for 4% -> 3%
where the time goes in v2:
time: 52.9 us; the launch traced here: 52.6 us
  blocking collectives  35 us (66%)
  starting transfers between devices  8.19 us (15%)
  Pallas kernels  5.23 us (10%)
  waiting for transfers between devices  3.49 us (7%)
  between operations  0.66 us (1%)
    all_to_all x1, blocking collectives, body(): lax.all_to_all(message, 'context', 0, 0, axis_index_groups=rows, tiled=True)  19.6 us
    all_to_all x1, blocking collectives, body(): lax.all_to_all(message, 'context', 0, 0, axis_index_groups=columns, tiled...  15.3 us
    all_to_all x1, starting transfers between devices, body(): received = lax.all_to_all(message, 'channel', 0, 0, tiled=True)  8.19 us
    all_to_all x1, waiting for transfers between devices, body(): received = lax.all_to_all(message, 'channel', 0, 0, tiled=True)  3.49 us
    pallas_call x1, Pallas kernels, body(): pl.pallas_call(pre_kernel, out_shape=(f32(ROWS, 6 * SUBLANES, LANES), f32...  2.51 us
    pallas_call x1, Pallas kernels, body(): pl.pallas_call(post_kernel, out_shape=jax.ShapeDtypeStruct((CHANNELS, CHU...  1.32 us
  transfers between devices with their start and end apart: 1, of which 1 were waited for; matrix products, arithmetic and copies ran while one was open for 0% of the time, Pallas kernels for 3%

profile of v2, /device:TPU:1, one launch (start us, length us, event | category | flops | bytes accessed | tf_op | source)
XLA Modules:
  0.0 52.6 jit_solution(12131434503003656342)
XLA Ops:
  0.6 2.5 %pre.1 = (f32[8,48,128]{2,1,0:T(8,128)S(1)}, f32[16,8,128]{2,1,0:T(8,128)S(1)}, f32[256,128]{1,0:T(8,128)S(1)}, f32[8,128]{1,0:T(8,128)S(1)}) custom-call(s32[1]{0:T(128)} %bitcast._.at_ref, bf16[64,512]{1,0:T(8,128)(2,1)} %x_hbm.1, bf16[64,512]{1,0:T(8,128)(2,1)} %g_hbm.1, f32[16,64]{1,0:T(8,128)} %bitcast.17), custom_call_target="tpu_custom_call" | custom-call | tf_op jit(solution)/shard_map/pre/pallas_call | solution.py:252
  3.2 19.6 %all_to_all.15.recv_ref = f32[8,48,128]{2,1,0:T(8,128)S(1)} all-to-all(f32[8,48,128]{2,1,0:T(8,128)S(1)} %get-tuple-element.15), channel_id=1, replica_groups={{0,8,16,24,32,40,48,56},{64,72,80,88,96,104,112,120},{128,136,144,152,1..., dimensions={0} | all-to-all | bytes 393216 | tf_op jit(solution)/shard_map/all_to_all | solution.py:270
  22.8 15.3 %all_to_all.16.recv_ref = f32[8,48,128]{2,1,0:T(8,128)S(1)} all-to-all(f32[8,48,128]{2,1,0:T(8,128)S(1)} %get-tuple-element.17), channel_id=1, replica_groups={{0,64,128,192,256,320,384,448},{8,72,136,200,264,328,392,456},{16,80,14..., dimensions={0} | all-to-all | bytes 393216 | tf_op jit(solution)/shard_map/all_to_all | solution.py:279
  38.2 0.7 %column.1 = (f32[8,16,128]{2,1,0:T(8,128)}, f32[8,128]{1,0:T(8,128)S(1)}) custom-call(s32[1]{0:T(128)} %bitcast._.at_ref, f32[8,48,128]{2,1,0:T(8,128)S(1)} %all_to_all.16.recv_ref, f32[8,128]{1,0:T(8,128)S(1)} %get-tuple-element.16.rate_ref, f32[8,128]{1,0:T(8,128)S(1)} %get-tuple-element.18.arrive_ref), custom_call_target="tpu_custom_call" | custom-call | tf_op jit(solution)/shard_map/column/pallas_call | solution.py:280
  38.9 0.0 copy-start
  38.9 0.0 copy-start.1
  38.9 8.2 %all-to-all-start.2 = ((f32[8,16,128]{2,1,0:T(8,128)}), f32[8,16,128]{2,1,0:T(8,128)S(1)}, u32[]{:S(2)}, u32[]{:S(2)}) async-start(f32[8,16,128]{2,1,0:T(8,128)} %get-tuple-element.20), calls=%async_computation.2 | async-start | bytes 131072 | tf_op jit(solution)/shard_map/all_to_all | solution.py:288
  47.1 0.0 copy-done
  47.1 0.0 copy-done.1
  47.1 1.3 %post.1 = bf16[64,512]{1,0:T(8,128)(2,1)} custom-call(f32[256,128]{1,0:T(8,128)S(1)} %get-tuple-element.13.gt_ref, f32[16,64]{1,0:T(8,128)S(1)} %bitcast.18, f32[16,64]{1,0:T(8,128)S(1)} %get-tuple-element.25.weight_ref, f32[16,8,128]{2,1,0:T(8,128)S(1)} %get-tuple-element.14.ain_ref, f32[8,128]{1,0:T(8,128)S(1)} %get-tuple-element.19.state_ref), custom_call_target="tpu_custom_call" | custom-call | tf_op jit(solution)/shard_map/post/pallas_call | solution.py:292
  48.4 3.5 %all-to-all-done.2.recv_ref = f32[8,16,128]{2,1,0:T(8,128)S(1)} async-done(((f32[8,16,128]{2,1,0:T(8,128)}), f32[8,16,128]{2,1,0:T(8,128)S(1)}, u32[]{:S(2)}, u32[]{:S(2)}) %all-to-all-start.2) | async-done | bytes 65568 | tf_op jit(solution)/shard_map/all_to_all | solution.py:288
  51.9 0.7 %final.1 = (f32[16,64]{1,0:T(8,128)}, f32[16,64]{1,0:T(8,128)}) custom-call(f32[8,16,128]{2,1,0:T(8,128)S(1)} %all-to-all-done.2.recv_ref, f32[16,64]{1,0:T(8,128)S(1)} %get-tuple-element.26.one_ref, f32[16,64]{1,0:T(8,128)S(1)} %get-tuple-element.24.two_ref, f32[16,64]{1,0:T(8,128)S(1)} %get-tuple-element.23.three_ref), custom_call_target="tpu_custom_call" | custom-call | tf_op jit(solution)/shard_map/final/pallas_call | solution.py:303
  (2 shorter events, 0.1 us)
Async XLA Ops:
  38.9 8.2 %copy-start = (f32[64,16]{0,1:T(8,128)S(1)}, f32[64,16]{0,1:T(8,128)}, u32[]{:S(2)}) copy-start(f32[64,16]{0,1:T(8,128)} %param.6) | copy-start | bytes 12292
  38.9 8.2 %copy-start.1 = (f32[64,16]{0,1:T(8,128)S(1)}, f32[64,16]{0,1:T(8,128)}, u32[]{:S(2)}) copy-start(f32[64,16]{0,1:T(8,128)} %param.7) | copy-start | bytes 12292
  38.9 13.0 %all-to-all-start.2 = ((f32[8,16,128]{2,1,0:T(8,128)}), f32[8,16,128]{2,1,0:T(8,128)S(1)}, u32[]{:S(2)}, u32[]{:S(2)}) async-start(f32[8,16,128]{2,1,0:T(8,128)} %get-tuple-element.20), calls=%async_computation.2 | async-start | bytes 131072 | tf_op jit(solution)/shard_map/all_to_all | solution.py:288

commit v3 on v2

v3 whole, which is shorter than its diff:
```python
import functools
import math

import jax
import jax.numpy as jnp
from jax import lax
from jax.experimental import pallas as pl
from jax.experimental.pallas import tpu as pltpu
from jax.sharding import PartitionSpec as P

LANES = 128
SUBLANES = 8
CHANNELS = 64
POLES = 16
STEP = 32
HALF = SUBLANES * STEP
CHUNK = 2 * HALF
BLOCKS = 4
BLOCK = HALF // BLOCKS
UNROLL = 4
ROWS = 8
GROUP = 8
GRANT = pltpu.CompilerParams(vmem_limit_bytes=8 << 20)


def low_half(shape):
    return lax.broadcasted_iota(jnp.int32, shape, len(shape) - 1) < CHANNELS


def double(rows):
    return jnp.concatenate([rows, rows], axis=1)


def pack(ref):
    even = ref[pl.ds(0, SUBLANES, stride=2), :]
    odd = ref[pl.ds(1, SUBLANES, stride=2), :]
    return jnp.where(low_half(even.shape), even, odd)


def transposed(block):
    stacked = jnp.concatenate([block[:, :HALF], block[:, HALF:]], axis=0)
    return stacked.astype(jnp.float32).T


def pre_kernel(_, x_hbm, g_hbm, rate_hbm, msg_ref, gt_ref, packed_ref, x_ref, g_ref, rate_ref, xt_ref, rows_ref, sems):
    copies = [
        pltpu.make_async_copy(source, target, sems.at[i])
        for i, (source, target) in enumerate(((rate_hbm, rate_ref), (g_hbm, g_ref), (x_hbm, x_ref)))
    ]
    for copy in copies:
        copy.start()
    copies[0].wait()
    rate = double(rate_ref[...])
    rows_ref[0] = rate
    packed_ref[...] = pack(rows_ref.at[0])
    decay = jnp.exp(-rate)
    copies[1].wait()
    gt_ref[...] = transposed(g_ref[...])
    copies[2].wait()
    xt_ref[...] = transposed(x_ref[...])

    def steps(outer, carry):
        total, slope, state, lean, value, tilt = (list(part) for part in carry)
        for inner in range(UNROLL):
            for b in range(BLOCKS):
                up = pl.ds(b * BLOCK + outer * UNROLL + inner, 1)
                down = pl.ds((b + 1) * BLOCK - 1 - outer * UNROLL - inner, 1)
                g, x, earlier = gt_ref[down, :], xt_ref[down, :], xt_ref[up, :]
                slope[b] = decay * (slope[b] + total[b])
                total[b] = decay * total[b] + g
                value[b % 2] = value[b % 2] + x * total[b]
                tilt[b % 2] = tilt[b % 2] + x * slope[b]
                state[b] = decay * (state[b] + earlier)
                lean[b] = decay * lean[b] + state[b]
        return total, slope, state, lean, value, tilt

    zero = jnp.zeros((POLES, LANES), jnp.float32)
    blank = [zero] * BLOCKS
    total, slope, state, lean, value, tilt = lax.fori_loop(
        0, BLOCK // UNROLL, steps, (blank, blank, blank, blank, [zero] * 2, [zero] * 2)
    )
    value = value[0] + value[1]
    tilt = tilt[0] + tilt[1]
    reach = jnp.exp(-float(BLOCK) * rate)
    coming, coming_slope = total[-1], slope[-1]
    behind, behind_lean = state[0], lean[0]
    for b in range(1, BLOCKS):
        back = BLOCKS - 1 - b
        value = value + state[back] * coming
        tilt = tilt + lean[back] * coming + state[back] * coming_slope
        coming_slope = slope[back] + reach * (coming_slope + float(BLOCK) * coming)
        coming = total[back] + reach * coming
        behind_lean = lean[b] + reach * (behind_lean + float(BLOCK) * behind)
        behind = state[b] + reach * behind
    low = low_half(zero.shape)
    turn = lambda v: pltpu.roll(v, CHANNELS, 1)
    late, late_slope = turn(coming), turn(coming_slope)
    value = value + jnp.where(low, behind * late, 0.0)
    tilt = tilt + jnp.where(low, behind_lean * late + behind * late_slope, 0.0)
    jump = jnp.exp(-float(HALF) * rate)
    sums = (
        coming + jump * late,
        coming_slope + jump * (late_slope + float(HALF) * late),
        jump * behind + turn(behind),
        jump * (behind_lean + float(HALF) * behind) + turn(behind_lean),
    )
    whole = [jnp.where(low, v, turn(v)) for v in sums] + [v + turn(v) for v in (value, tilt)]
    for q, v in enumerate(whole):
        rows_ref[q] = v
        packed = pack(rows_ref.at[q])
        for d in range(ROWS):
            msg_ref[d, pl.ds(q * SUBLANES, SUBLANES), :] = packed


def combine(recv_ref, rate, span):
    part = lambda d, q: recv_ref[d, pl.ds(q * SUBLANES, SUBLANES), :]
    decay = jnp.exp(-span * rate)
    coming = jnp.zeros_like(rate)
    coming_slope = jnp.zeros_like(rate)
    value = part(ROWS - 1, 4)
    tilt = part(ROWS - 1, 5)
    arriving = [coming] * ROWS
    for d in reversed(range(ROWS - 1)):
        coming_slope = part(d + 1, 1) + decay * (coming_slope + span * coming)
        coming = part(d + 1, 0) + decay * coming
        arriving[d] = coming
        value = value + part(d, 4) + part(d, 2) * coming
        tilt = tilt + part(d, 5) + part(d, 3) * coming + part(d, 2) * coming_slope
    slope = part(0, 1) + decay * (coming_slope + span * coming)
    total = part(0, 0) + decay * coming
    state = part(0, 2)
    lean = part(0, 3)
    for d in range(1, ROWS):
        lean = part(d, 3) + decay * (lean + span * state)
        state = part(d, 2) + decay * state
    return total, slope, state, lean, value, tilt, arriving


def pick(at, choices):
    out = choices[0]
    for d in range(1, ROWS):
        out = jnp.where(at == d, choices[d], out)
    return out


def row_kernel(at_ref, recv_ref, rate_ref, msg_ref, arrive_ref):
    rate = rate_ref[...]
    *sums, arriving = combine(recv_ref, rate, float(CHUNK))
    for q, packed in enumerate(sums):
        for d in range(ROWS):
            msg_ref[d, pl.ds(q * SUBLANES, SUBLANES), :] = packed
    arrive_ref[...] = pick(lax.rem(at_ref[0], ROWS), arriving)


def column_kernel(at_ref, recv_ref, rate_ref, arrive_ref, msg_ref, state_ref):
    rate = rate_ref[...]
    sums = combine(recv_ref, rate, float(CHUNK * ROWS))
    for q in range(2):
        for d in range(GROUP):
            msg_ref[d, pl.ds(q * SUBLANES, SUBLANES), :] = sums[4 + q]
    after = float(CHUNK) * (ROWS - 1 - lax.rem(at_ref[0], ROWS)).astype(jnp.float32)
    state_ref[...] = arrive_ref[...] + jnp.exp(-after * rate) * pick(lax.div(at_ref[0], ROWS), sums[6])


def post_kernel(gt_ref, rate_ref, weight_ref, state_ref, out_ref, yt_ref):
    full = (SUBLANES, LANES)
    low = low_half(full)
    low_row = low_half((1, LANES))
    block = lax.broadcasted_iota(jnp.int32, full, 0)
    after = float(STEP) * (SUBLANES - 1 - block).astype(jnp.float32)
    away = jnp.where(low, after + float(HALF), after)
    rates = double(rate_ref[...])
    weights = double(weight_ref[...])
    decays = jnp.exp(-rates)
    spans = jnp.exp(-float(STEP) * rates)
    wide = lambda rows, k: jnp.broadcast_to(rows[k : k + 1], full)
    for first in range(0, POLES, 8):
        poles = range(first, first + 8)
        decay = [wide(decays, k) for k in poles]

        def ends(at, total):
            g = gt_ref[pl.ds(STEP - 1 - at, SUBLANES, stride=STEP), :]
            return [decay[i] * total[i] + g for i in range(8)]

        blank = [jnp.zeros(full, jnp.float32)] * 8
        local = lax.fori_loop(0, STEP, ends, blank, unroll=4)
        entry = []
        for i, k in enumerate(poles):
            total = local[i]
            far = wide(spans, k)
            for shift in (1, 2, 4):
                moved = pltpu.roll(total, SUBLANES - shift, 0)
                total = total + jnp.where(block < SUBLANES - shift, far * moved, 0.0)
                far = far * far
            inside = jnp.where(block < SUBLANES - 1, pltpu.roll(total, SUBLANES - 1, 0), 0.0)
            late = jnp.where(low, pltpu.roll(jnp.broadcast_to(total[0:1], full), CHANNELS, 1), 0.0)
            row = state_ref[pl.ds(k // 2, 1), :]
            other = pltpu.roll(row, CHANNELS, 1)
            both = jnp.where(low_row, row, other) if k % 2 == 0 else jnp.where(low_row, other, row)
            rate = rates[k : k + 1]
            entry.append(inside + jnp.exp(-after * rate) * late + jnp.exp(-away * rate) * both)
        weight = [wide(weights, k) for k in poles]

        def outputs(at, total):
            rows = pl.ds(STEP - 1 - at, SUBLANES, stride=STEP)
            g = gt_ref[rows, :]
            total = [decay[i] * total[i] + g for i in range(8)]
            terms = [weight[i] * total[i] for i in range(8)]
            while len(terms) > 1:
                terms = [terms[i] + terms[i + 1] for i in range(0, len(terms), 2)]
            yt_ref[rows, :] = terms[0] if first == 0 else yt_ref[rows, :] + terms[0]
            return total

        lax.fori_loop(0, STEP, outputs, entry, unroll=4)
    stacked = yt_ref[...].T
    out_ref[:, :HALF] = stacked[:CHANNELS].astype(jnp.bfloat16)
    out_ref[:, HALF:] = stacked[CHANNELS:].astype(jnp.bfloat16)


def final_kernel(recv_ref, one_ref, two_ref, three_ref, res_ref, log_ref):
    value = recv_ref[0, pl.ds(0, SUBLANES), :]
    tilt = recv_ref[0, pl.ds(SUBLANES, SUBLANES), :]
    for d in range(1, GROUP):
        value = value + recv_ref[d, pl.ds(0, SUBLANES), :]
        tilt = tilt + recv_ref[d, pl.ds(SUBLANES, SUBLANES), :]
    for k in range(POLES):
        lanes = slice(0, CHANNELS) if k % 2 == 0 else slice(CHANNELS, LANES)
        first = value[k // 2 : k // 2 + 1, lanes]
        second = tilt[k // 2 : k // 2 + 1, lanes]
        at = pl.ds(k, 1)
        res_ref[at, :] = one_ref[at, :] * first
        log_ref[at, :] = two_ref[at, :] * first - three_ref[at, :] * second


def vmem(count):
    return [pl.BlockSpec(memory_space=pltpu.VMEM)] * count


def f32(*shape):
    return jax.ShapeDtypeStruct(shape, jnp.float32)


def scratch(*shape):
    return pltpu.VMEM(shape, jnp.float32)


def body(inputs, grad_out, decay_rates, residues):
    rate = decay_rates.T
    residue = residues.T
    at = lax.axis_index("context").astype(jnp.int32).reshape(1)
    rows = [[y * ROWS + z for z in range(ROWS)] for y in range(ROWS)]
    columns = [[y * ROWS + z for y in range(ROWS)] for z in range(ROWS)]
    smem = [pl.BlockSpec(memory_space=pltpu.SMEM)]

    message, turned, packed = pl.pallas_call(
        pre_kernel,
        out_shape=(f32(ROWS, 6 * SUBLANES, LANES), f32(HALF, LANES), f32(SUBLANES, LANES)),
        in_specs=smem + [pl.BlockSpec(memory_space=pltpu.HBM)] * 3,
        out_specs=tuple(vmem(3)),
        scratch_shapes=[
            pltpu.VMEM((CHANNELS, CHUNK), jnp.bfloat16),
            pltpu.VMEM((CHANNELS, CHUNK), jnp.bfloat16),
            scratch(POLES, CHANNELS),
            scratch(HALF, LANES),
            scratch(6, POLES, LANES),
            pltpu.SemaphoreType.DMA((3,)),
        ],
        compiler_params=GRANT,
        name="pre",
    )(at, *(pltpu.with_memory_space_constraint(v, pltpu.HBM) for v in (inputs, grad_out, rate)))
    received = lax.all_to_all(message, "context", 0, 0, axis_index_groups=rows, tiled=True)
    message, arrived = pl.pallas_call(
        row_kernel,
        out_shape=(f32(ROWS, 6 * SUBLANES, LANES), f32(SUBLANES, LANES)),
        in_specs=smem + vmem(2),
        out_specs=tuple(vmem(2)),
        compiler_params=GRANT,
        name="row",
    )(at, received, packed)
    received = lax.all_to_all(message, "context", 0, 0, axis_index_groups=columns, tiled=True)
    message, state = pl.pallas_call(
        column_kernel,
        out_shape=(f32(GROUP, 2 * SUBLANES, LANES), f32(SUBLANES, LANES)),
        in_specs=smem + vmem(3),
        out_specs=tuple(vmem(2)),
        compiler_params=GRANT,
        name="column",
    )(at, received, packed, arrived)
    received = lax.all_to_all(message, "channel", 0, 0, tiled=True)

    gain = jnp.sqrt(-jnp.expm1(-2.0 * rate))
    decay = jnp.exp(-rate)
    grad_in = pl.pallas_call(
        post_kernel,
        out_shape=jax.ShapeDtypeStruct((CHANNELS, CHUNK), jnp.bfloat16),
        in_specs=vmem(4),
        out_specs=vmem(1)[0],
        scratch_shapes=[scratch(HALF, LANES)],
        compiler_params=GRANT,
        name="post",
    )(turned, rate, residue * gain, state)
    norm = 1.0 / math.sqrt(CHUNK * ROWS * ROWS * GROUP)
    scaled = residue * rate * norm
    res_grad, log_grad = pl.pallas_call(
        final_kernel,
        out_shape=(f32(POLES, CHANNELS), f32(POLES, CHANNELS)),
        in_specs=vmem(4),
        out_specs=tuple(vmem(2)),
        compiler_params=GRANT,
        name="final",
    )(received, gain * norm, scaled * (decay * decay / gain), scaled * gain)
    return (grad_in, res_grad.T, log_grad.T)


def solution(mesh):
    return jax.shard_map(
        body,
        mesh=mesh,
        in_specs=(P("channel", "context"), P("channel", "context"), P(), P()),
        out_specs=(P("channel", "context"), P(), P()),
        check_vma=False,
    )
```

time: 52.9 us -> 52.7 us (level)
  waiting for transfers between devices: 3.49 us -> 2.64 us
  Pallas kernels: 5.23 us -> 5.86 us
    all_to_all x1, waiting for transfers between devices: 3.49 us -> 2.64 us  [body(): received = lax.all_to_all(message, 'channel', 0, 0, tiled=True)]
    pallas_call x1, Pallas kernels: 1.32 us -> 2.17 us  [body(): pl.pallas_call(post_kernel, out_shape=jax.ShapeDtypeStruct((CHANNELS, CHU...]
  transfers between devices with their start and end apart: 1 -> 1, of which waited for: 1 -> 1; matrix products, arithmetic and copies ran while one was open for 0% -> 0% of each run, Pallas kernels for 3% -> 4%
where the time goes in v3:
time: 52.7 us; the launch traced here: 52.4 us
  blocking collectives  35 us (66%)
  starting transfers between devices  8.19 us (16%)
  Pallas kernels  5.86 us (11%)
  waiting for transfers between devices  2.64 us (5%)
  between operations  0.66 us (1%)
    all_to_all x1, blocking collectives, body(): lax.all_to_all(message, 'context', 0, 0, axis_index_groups=rows, tiled=True)  19.6 us
    all_to_all x1, blocking collectives, body(): lax.all_to_all(message, 'context', 0, 0, axis_index_groups=columns, tiled...  15.3 us
    all_to_all x1, starting transfers between devices, body(): received = lax.all_to_all(message, 'channel', 0, 0, tiled=True)  8.19 us
    all_to_all x1, waiting for transfers between devices, body(): received = lax.all_to_all(message, 'channel', 0, 0, tiled=True)  2.64 us
    pallas_call x1, Pallas kernels, body(): pl.pallas_call(pre_kernel, out_shape=(f32(ROWS, 6 * SUBLANES, LANES), f32...  2.29 us
    pallas_call x1, Pallas kernels, body(): pl.pallas_call(post_kernel, out_shape=jax.ShapeDtypeStruct((CHANNELS, CHU...  2.17 us
  transfers between devices with their start and end apart: 1, of which 1 were waited for; matrix products, arithmetic and copies ran while one was open for 0% of the time, Pallas kernels for 4%

profile of v3, /device:TPU:1, one launch (start us, length us, event | category | flops | bytes accessed | tf_op | source)
XLA Modules:
  0.0 52.4 jit_solution(3622219035791671284)
XLA Ops:
  0.6 2.3 %pre.1 = (f32[8,48,128]{2,1,0:T(8,128)S(1)}, f32[256,128]{1,0:T(8,128)S(1)}, f32[8,128]{1,0:T(8,128)S(1)}) custom-call(s32[1]{0:T(128)} %bitcast._.at_ref, bf16[64,512]{1,0:T(8,128)(2,1)} %x_hbm.1, bf16[64,512]{1,0:T(8,128)(2,1)} %g_hbm.1, f32[16,64]{1,0:T(8,128)} %bitcast.17), custom_call_target="tpu_custom_call" | custom-call | tf_op jit(solution)/shard_map/pre/pallas_call | solution.py:255
  2.9 19.6 %all_to_all.15.recv_ref = f32[8,48,128]{2,1,0:T(8,128)S(1)} all-to-all(f32[8,48,128]{2,1,0:T(8,128)S(1)} %get-tuple-element.13), channel_id=1, replica_groups={{0,8,16,24,32,40,48,56},{64,72,80,88,96,104,112,120},{128,136,144,152,1..., dimensions={0} | all-to-all | bytes 393216 | tf_op jit(solution)/shard_map/all_to_all | solution.py:271
  22.6 15.3 %all_to_all.16.recv_ref = f32[8,48,128]{2,1,0:T(8,128)S(1)} all-to-all(f32[8,48,128]{2,1,0:T(8,128)S(1)} %get-tuple-element.15), channel_id=1, replica_groups={{0,64,128,192,256,320,384,448},{8,72,136,200,264,328,392,456},{16,80,14..., dimensions={0} | all-to-all | bytes 393216 | tf_op jit(solution)/shard_map/all_to_all | solution.py:280
  38.0 0.7 %column.1 = (f32[8,16,128]{2,1,0:T(8,128)}, f32[8,128]{1,0:T(8,128)S(1)}) custom-call(s32[1]{0:T(128)} %bitcast._.at_ref, f32[8,48,128]{2,1,0:T(8,128)S(1)} %all_to_all.16.recv_ref, f32[8,128]{1,0:T(8,128)S(1)} %get-tuple-element.14.rate_ref, f32[8,128]{1,0:T(8,128)S(1)} %get-tuple-element.16.arrive_ref), custom_call_target="tpu_custom_call" | custom-call | tf_op jit(solution)/shard_map/column/pallas_call | solution.py:281
  38.6 0.0 copy-start
  38.6 0.0 copy-start.1
  38.6 8.2 %all-to-all-start.2 = ((f32[8,16,128]{2,1,0:T(8,128)}), f32[8,16,128]{2,1,0:T(8,128)S(1)}, u32[]{:S(2)}, u32[]{:S(2)}) async-start(f32[8,16,128]{2,1,0:T(8,128)} %get-tuple-element.18), calls=%async_computation.2 | async-start | bytes 131072 | tf_op jit(solution)/shard_map/all_to_all | solution.py:289
  46.8 0.0 copy-done
  46.8 0.0 copy-done.1
  46.9 2.2 %post.1 = bf16[64,512]{1,0:T(8,128)(2,1)} custom-call(f32[256,128]{1,0:T(8,128)S(1)} %get-tuple-element.12.gt_ref, f32[16,64]{1,0:T(8,128)S(1)} %bitcast.18, f32[16,64]{1,0:T(8,128)S(1)} %get-tuple-element.23.weight_ref, f32[8,128]{1,0:T(8,128)S(1)} %get-tuple-element.17.state_ref), custom_call_target="tpu_custom_call" | custom-call | tf_op jit(solution)/shard_map/post/pallas_call | solution.py:293
  49.0 2.6 %all-to-all-done.2.recv_ref = f32[8,16,128]{2,1,0:T(8,128)S(1)} async-done(((f32[8,16,128]{2,1,0:T(8,128)}), f32[8,16,128]{2,1,0:T(8,128)S(1)}, u32[]{:S(2)}, u32[]{:S(2)}) %all-to-all-start.2) | async-done | bytes 65568 | tf_op jit(solution)/shard_map/all_to_all | solution.py:289
  51.7 0.7 %final.1 = (f32[16,64]{1,0:T(8,128)}, f32[16,64]{1,0:T(8,128)}) custom-call(f32[8,16,128]{2,1,0:T(8,128)S(1)} %all-to-all-done.2.recv_ref, f32[16,64]{1,0:T(8,128)S(1)} %get-tuple-element.24.one_ref, f32[16,64]{1,0:T(8,128)S(1)} %get-tuple-element.22.two_ref, f32[16,64]{1,0:T(8,128)S(1)} %get-tuple-element.21.three_ref), custom_call_target="tpu_custom_call" | custom-call | tf_op jit(solution)/shard_map/final/pallas_call | solution.py:304
  (2 shorter events, 0.1 us)
Async XLA Ops:
  38.6 8.2 %copy-start = (f32[64,16]{0,1:T(8,128)S(1)}, f32[64,16]{0,1:T(8,128)}, u32[]{:S(2)}) copy-start(f32[64,16]{0,1:T(8,128)} %param.6) | copy-start | bytes 12292
  38.6 8.2 %copy-start.1 = (f32[64,16]{0,1:T(8,128)S(1)}, f32[64,16]{0,1:T(8,128)}, u32[]{:S(2)}) copy-start(f32[64,16]{0,1:T(8,128)} %param.7) | copy-start | bytes 12292
  38.6 13.0 %all-to-all-start.2 = ((f32[8,16,128]{2,1,0:T(8,128)}), f32[8,16,128]{2,1,0:T(8,128)S(1)}, u32[]{:S(2)}, u32[]{:S(2)}) async-start(f32[8,16,128]{2,1,0:T(8,128)} %get-tuple-element.18), calls=%async_computation.2 | async-start | bytes 131072 | tf_op jit(solution)/shard_map/all_to_all | solution.py:289

commit v4 on v3

--- a/solution.py
+++ b/solution.py
@@ -17,9 +17,12 @@
 CHUNK = 2 * HALF
 BLOCKS = 4
 BLOCK = HALF // BLOCKS
-UNROLL = 4
+UNROLL = 16
 ROWS = 8
 GROUP = 8
+ROW_ORDER = [7, 6, 5, 4, 3, 2, 1, 0]
+COLUMN_ORDER = [4, 3, 2, 1, 0, 7, 6, 5]
+CHANNEL_ORDER = [5, 4, 3, 2, 1, 0, 7, 6]
 GRANT = pltpu.CompilerParams(vmem_limit_bytes=8 << 20)
 
 
@@ -112,8 +115,8 @@
             msg_ref[d, pl.ds(q * SUBLANES, SUBLANES), :] = packed
 
 
-def combine(recv_ref, rate, span):
-    part = lambda d, q: recv_ref[d, pl.ds(q * SUBLANES, SUBLANES), :]
+def combine(recv_ref, rate, span, order):
+    part = lambda d, q: recv_ref[order.index(d), pl.ds(q * SUBLANES, SUBLANES), :]
     decay = jnp.exp(-span * rate)
     coming = jnp.zeros_like(rate)
     coming_slope = jnp.zeros_like(rate)
@@ -145,7 +148,7 @@
 
 def row_kernel(at_ref, recv_ref, rate_ref, msg_ref, arrive_ref):
     rate = rate_ref[...]
-    *sums, arriving = combine(recv_ref, rate, float(CHUNK))
+    *sums, arriving = combine(recv_ref, rate, float(CHUNK), ROW_ORDER)
     for q, packed in enumerate(sums):
         for d in range(ROWS):
             msg_ref[d, pl.ds(q * SUBLANES, SUBLANES), :] = packed
@@ -154,7 +157,7 @@
 
 def column_kernel(at_ref, recv_ref, rate_ref, arrive_ref, msg_ref, state_ref):
     rate = rate_ref[...]
-    sums = combine(recv_ref, rate, float(CHUNK * ROWS))
+    sums = combine(recv_ref, rate, float(CHUNK * ROWS), COLUMN_ORDER)
     for q in range(2):
         for d in range(GROUP):
             msg_ref[d, pl.ds(q * SUBLANES, SUBLANES), :] = sums[4 + q]
@@ -244,18 +247,11 @@
     return pltpu.VMEM(shape, jnp.float32)
 
 
-def body(inputs, grad_out, decay_rates, residues):
-    rate = decay_rates.T
-    residue = residues.T
-    at = lax.axis_index("context").astype(jnp.int32).reshape(1)
-    rows = [[y * ROWS + z for z in range(ROWS)] for y in range(ROWS)]
-    columns = [[y * ROWS + z for y in range(ROWS)] for z in range(ROWS)]
-    smem = [pl.BlockSpec(memory_space=pltpu.SMEM)]
-
-    message, turned, packed = pl.pallas_call(
+def first_call(at, x, g, rate, name="pre"):
+    return pl.pallas_call(
         pre_kernel,
         out_shape=(f32(ROWS, 6 * SUBLANES, LANES), f32(HALF, LANES), f32(SUBLANES, LANES)),
-        in_specs=smem + [pl.BlockSpec(memory_space=pltpu.HBM)] * 3,
+        in_specs=[pl.BlockSpec(memory_space=pltpu.SMEM)] + [pl.BlockSpec(memory_space=pltpu.HBM)] * 3,
         out_specs=tuple(vmem(3)),
         scratch_shapes=[
             pltpu.VMEM((CHANNELS, CHUNK), jnp.bfloat16),
@@ -266,8 +262,21 @@
             pltpu.SemaphoreType.DMA((3,)),
         ],
         compiler_params=GRANT,
-        name="pre",
-    )(at, *(pltpu.with_memory_space_constraint(v, pltpu.HBM) for v in (inputs, grad_out, rate)))
+        name=name,
+    )(at, x, g, rate)
+
+
+def body(inputs, grad_out, decay_rates, residues):
+    rate = decay_rates.T
+    residue = residues.T
+    at = lax.axis_index("context").astype(jnp.int32).reshape(1)
+    rows = [[y * ROWS + z for z in ROW_ORDER] for y in range(ROWS)]
+    columns = [[y * ROWS + z for y in COLUMN_ORDER] for z in range(ROWS)]
+    smem = [pl.BlockSpec(memory_space=pltpu.SMEM)]
+
+    message, turned, packed = first_call(
+        at, *(pltpu.with_memory_space_constraint(v, pltpu.HBM) for v in (inputs, grad_out, rate))
+    )
     received = lax.all_to_all(message, "context", 0, 0, axis_index_groups=rows, tiled=True)
     message, arrived = pl.pallas_call(
         row_kernel,
@@ -286,7 +295,7 @@
         compiler_params=GRANT,
         name="column",
     )(at, received, packed, arrived)
-    received = lax.all_to_all(message, "channel", 0, 0, tiled=True)
+    received = lax.all_to_all(message, "channel", 0, 0, axis_index_groups=[CHANNEL_ORDER], tiled=True)
 
     gain = jnp.sqrt(-jnp.expm1(-2.0 * rate))
     decay = jnp.exp(-rate)

time: 52.7 us -> 44 us (0.83)
  blocking collectives: 35 us -> 28.9 us
  waiting for transfers between devices: 2.64 us -> 0.53 us
    all_to_all x1, blocking collectives: 15.3 us -> 11.5 us  [body(): lax.all_to_all(message, 'context', 0, 0, axis_index_groups=columns, tiled...]
    all_to_all x1, blocking collectives: 19.6 us -> 17.4 us  [body(): lax.all_to_all(message, 'context', 0, 0, axis_index_groups=rows, tiled=True)]
    all_to_all x1, waiting for transfers between devices: 2.64 us -> 0.53 us  [body(): lax.all_to_all(message, 'channel', 0, 0, axis_index_groups=[CHANNEL_ORDER...]
  transfers between devices with their start and end apart: 1 -> 1, of which waited for: 1 -> 1; matrix products, arithmetic and copies ran while one was open for 0% -> 0% of each run, Pallas kernels for 4% -> 5%
where the time goes in v4:
time: 44 us; the launch traced here: 43.7 us
  blocking collectives  28.9 us (66%)
  starting transfers between devices  7.87 us (18%)
  Pallas kernels  5.7 us (13%)
  between operations  0.66 us (2%)
  waiting for transfers between devices  0.53 us (1%)
    all_to_all x1, blocking collectives, body(): lax.all_to_all(message, 'context', 0, 0, axis_index_groups=rows, tiled=True)  17.4 us
    all_to_all x1, blocking collectives, body(): lax.all_to_all(message, 'context', 0, 0, axis_index_groups=columns, tiled...  11.5 us
    all_to_all x1, starting transfers between devices, body(): lax.all_to_all(message, 'channel', 0, 0, axis_index_groups=[CHANNEL_ORDER...  7.87 us
    pallas_call x1, Pallas kernels, body(): pl.pallas_call(post_kernel, out_shape=jax.ShapeDtypeStruct((CHANNELS, CHU...  2.17 us
    pallas_call x1, Pallas kernels, first_call(): pl.pallas_call(pre_kernel, out_shape=(f32(ROWS, 6 * SUBLANES, LANES), f32...  2.13 us
  transfers between devices with their start and end apart: 1, of which 1 were waited for; matrix products, arithmetic and copies ran while one was open for 0% of the time, Pallas kernels for 5%

profile of v4, /device:TPU:1, one launch (start us, length us, event | category | flops | bytes accessed | tf_op | source)
XLA Modules:
  0.0 43.7 jit_solution(16170393425345571393)
XLA Ops:
  0.6 2.1 %pre.1 = (f32[8,48,128]{2,1,0:T(8,128)S(1)}, f32[256,128]{1,0:T(8,128)S(1)}, f32[8,128]{1,0:T(8,128)S(1)}) custom-call(s32[1]{0:T(128)} %bitcast._.at_ref, bf16[64,512]{1,0:T(8,128)(2,1)} %x_hbm.1, bf16[64,512]{1,0:T(8,128)(2,1)} %g_hbm.1, f32[16,64]{1,0:T(8,128)} %bitcast.17), custom_call_target="tpu_custom_call" | custom-call | tf_op jit(solution)/shard_map/pre/pallas_call | solution.py:251
  2.8 17.4 %all_to_all.15.recv_ref = f32[8,48,128]{2,1,0:T(8,128)S(1)} all-to-all(f32[8,48,128]{2,1,0:T(8,128)S(1)} %get-tuple-element.13), channel_id=1, replica_groups={{56,48,40,32,24,16,8,0},{120,112,104,96,88,80,72,64},{184,176,168,160,1..., dimensions={0} | all-to-all | bytes 393216 | tf_op jit(solution)/shard_map/all_to_all | solution.py:280
  20.2 11.5 %all_to_all.16.recv_ref = f32[8,48,128]{2,1,0:T(8,128)S(1)} all-to-all(f32[8,48,128]{2,1,0:T(8,128)S(1)} %get-tuple-element.15), channel_id=1, replica_groups={{256,192,128,64,0,448,384,320},{264,200,136,72,8,456,392,328},{272,208,..., dimensions={0} | all-to-all | bytes 393216 | tf_op jit(solution)/shard_map/all_to_all | solution.py:289
  31.7 0.7 %column.1 = (f32[8,16,128]{2,1,0:T(8,128)}, f32[8,128]{1,0:T(8,128)S(1)}) custom-call(s32[1]{0:T(128)} %bitcast._.at_ref, f32[8,48,128]{2,1,0:T(8,128)S(1)} %all_to_all.16.recv_ref, f32[8,128]{1,0:T(8,128)S(1)} %get-tuple-element.14.rate_ref, f32[8,128]{1,0:T(8,128)S(1)} %get-tuple-element.16.arrive_ref), custom_call_target="tpu_custom_call" | custom-call | tf_op jit(solution)/shard_map/column/pallas_call | solution.py:290
  32.4 0.0 copy-start
  32.4 0.0 copy-start.1
  32.4 7.9 %all-to-all-start.2 = ((f32[8,16,128]{2,1,0:T(8,128)}), f32[8,16,128]{2,1,0:T(8,128)S(1)}, u32[]{:S(2)}, u32[]{:S(2)}) async-start(f32[8,16,128]{2,1,0:T(8,128)} %get-tuple-element.18), calls=%async_computation.2 | async-start | bytes 131072 | tf_op jit(solution)/shard_map/all_to_all | solution.py:298
  40.2 0.0 copy-done
  40.2 0.0 copy-done.1
  40.3 2.2 %post.1 = bf16[64,512]{1,0:T(8,128)(2,1)} custom-call(f32[256,128]{1,0:T(8,128)S(1)} %get-tuple-element.12.gt_ref, f32[16,64]{1,0:T(8,128)S(1)} %bitcast.18, f32[16,64]{1,0:T(8,128)S(1)} %get-tuple-element.23.weight_ref, f32[8,128]{1,0:T(8,128)S(1)} %get-tuple-element.17.state_ref), custom_call_target="tpu_custom_call" | custom-call | tf_op jit(solution)/shard_map/post/pallas_call | solution.py:302
  42.4 0.5 %all-to-all-done.2.recv_ref = f32[8,16,128]{2,1,0:T(8,128)S(1)} async-done(((f32[8,16,128]{2,1,0:T(8,128)}), f32[8,16,128]{2,1,0:T(8,128)S(1)}, u32[]{:S(2)}, u32[]{:S(2)}) %all-to-all-start.2) | async-done | bytes 65568 | tf_op jit(solution)/shard_map/all_to_all | solution.py:298
  43.0 0.7 %final.1 = (f32[16,64]{1,0:T(8,128)}, f32[16,64]{1,0:T(8,128)}) custom-call(f32[8,16,128]{2,1,0:T(8,128)S(1)} %all-to-all-done.2.recv_ref, f32[16,64]{1,0:T(8,128)S(1)} %get-tuple-element.24.one_ref, f32[16,64]{1,0:T(8,128)S(1)} %get-tuple-element.22.two_ref, f32[16,64]{1,0:T(8,128)S(1)} %get-tuple-element.21.three_ref), custom_call_target="tpu_custom_call" | custom-call | tf_op jit(solution)/shard_map/final/pallas_call | solution.py:313
  (2 shorter events, 0.1 us)
Async XLA Ops:
  32.4 7.9 %copy-start = (f32[64,16]{0,1:T(8,128)S(1)}, f32[64,16]{0,1:T(8,128)}, u32[]{:S(2)}) copy-start(f32[64,16]{0,1:T(8,128)} %param.6) | copy-start | bytes 12292
  32.4 7.9 %copy-start.1 = (f32[64,16]{0,1:T(8,128)S(1)}, f32[64,16]{0,1:T(8,128)}, u32[]{:S(2)}) copy-start(f32[64,16]{0,1:T(8,128)} %param.7) | copy-start | bytes 12292
  32.4 10.6 %all-to-all-start.2 = ((f32[8,16,128]{2,1,0:T(8,128)}), f32[8,16,128]{2,1,0:T(8,128)S(1)}, u32[]{:S(2)}, u32[]{:S(2)}) async-start(f32[8,16,128]{2,1,0:T(8,128)} %get-tuple-element.18), calls=%async_computation.2 | async-start | bytes 131072 | tf_op jit(solution)/shard_map/all_to_all | solution.py:298

commit v5 on v4

--- a/solution.py
+++ b/solution.py
@@ -18,9 +18,10 @@
 BLOCKS = 4
 BLOCK = HALF // BLOCKS
 UNROLL = 16
+POSTU = 8
 ROWS = 8
 GROUP = 8
-ROW_ORDER = [7, 6, 5, 4, 3, 2, 1, 0]
+ROW_ORDER = [6, 5, 4, 3, 2, 1, 0, 7]
 COLUMN_ORDER = [4, 3, 2, 1, 0, 7, 6, 5]
 CHANNEL_ORDER = [5, 4, 3, 2, 1, 0, 7, 6]
 GRANT = pltpu.CompilerParams(vmem_limit_bytes=8 << 20)
@@ -186,7 +187,7 @@
             return [decay[i] * total[i] + g for i in range(8)]
 
         blank = [jnp.zeros(full, jnp.float32)] * 8
-        local = lax.fori_loop(0, STEP, ends, blank, unroll=4)
+        local = lax.fori_loop(0, STEP, ends, blank, unroll=POSTU)
         entry = []
         for i, k in enumerate(poles):
             total = local[i]
@@ -214,7 +215,7 @@
             yt_ref[rows, :] = terms[0] if first == 0 else yt_ref[rows, :] + terms[0]
             return total
 
-        lax.fori_loop(0, STEP, outputs, entry, unroll=4)
+        lax.fori_loop(0, STEP, outputs, entry, unroll=POSTU)
     stacked = yt_ref[...].T
     out_ref[:, :HALF] = stacked[:CHANNELS].astype(jnp.bfloat16)
     out_ref[:, HALF:] = stacked[CHANNELS:].astype(jnp.bfloat16)

time: 44 us -> 43.2 us (0.982)
  blocking collectives: 28.9 us -> 28.3 us
    all_to_all x1, blocking collectives: 17.4 us -> 16.8 us  [body(): lax.all_to_all(message, 'context', 0, 0, axis_index_groups=rows, tiled=True)]
where the time goes in v5:
time: 43.2 us; the launch traced here: 42.8 us
  blocking collectives  28.3 us (66%)
  starting transfers between devices  7.66 us (18%)
  Pallas kernels  5.63 us (13%)
  between operations  0.66 us (2%)
  waiting for transfers between devices  0.59 us (1%)
    all_to_all x1, blocking collectives, body(): lax.all_to_all(message, 'context', 0, 0, axis_index_groups=rows, tiled=True)  16.8 us
    all_to_all x1, blocking collectives, body(): lax.all_to_all(message, 'context', 0, 0, axis_index_groups=columns, tiled...  11.5 us
    all_to_all x1, starting transfers between devices, body(): lax.all_to_all(message, 'channel', 0, 0, axis_index_groups=[CHANNEL_ORDER...  7.66 us
    pallas_call x1, Pallas kernels, first_call(): pl.pallas_call(pre_kernel, out_shape=(f32(ROWS, 6 * SUBLANES, LANES), f32...  2.13 us
    pallas_call x1, Pallas kernels, body(): pl.pallas_call(post_kernel, out_shape=jax.ShapeDtypeStruct((CHANNELS, CHU...  2.1 us
  transfers between devices with their start and end apart: 1, of which 1 were waited for; matrix products, arithmetic and copies ran while one was open for 0% of the time, Pallas kernels for 5%

profile of v5, /device:TPU:1, one launch (start us, length us, event | category | flops | bytes accessed | tf_op | source)
XLA Modules:
  0.0 42.8 jit_solution(16059953626325131282)
XLA Ops:
  0.6 2.1 %pre.1 = (f32[8,48,128]{2,1,0:T(8,128)S(1)}, f32[256,128]{1,0:T(8,128)S(1)}, f32[8,128]{1,0:T(8,128)S(1)}) custom-call(s32[1]{0:T(128)} %bitcast._.at_ref, bf16[64,512]{1,0:T(8,128)(2,1)} %x_hbm.1, bf16[64,512]{1,0:T(8,128)(2,1)} %g_hbm.1, f32[16,64]{1,0:T(8,128)} %bitcast.17), custom_call_target="tpu_custom_call" | custom-call | tf_op jit(solution)/shard_map/pre/pallas_call | solution.py:252
  2.8 16.8 %all_to_all.15.recv_ref = f32[8,48,128]{2,1,0:T(8,128)S(1)} all-to-all(f32[8,48,128]{2,1,0:T(8,128)S(1)} %get-tuple-element.13), channel_id=1, replica_groups={{48,40,32,24,16,8,0,56},{112,104,96,88,80,72,64,120},{176,168,160,152,1..., dimensions={0} | all-to-all | bytes 393216 | tf_op jit(solution)/shard_map/all_to_all | solution.py:281
  19.6 11.5 %all_to_all.16.recv_ref = f32[8,48,128]{2,1,0:T(8,128)S(1)} all-to-all(f32[8,48,128]{2,1,0:T(8,128)S(1)} %get-tuple-element.15), channel_id=1, replica_groups={{256,192,128,64,0,448,384,320},{264,200,136,72,8,456,392,328},{272,208,..., dimensions={0} | all-to-all | bytes 393216 | tf_op jit(solution)/shard_map/all_to_all | solution.py:290
  31.1 0.7 %column.1 = (f32[8,16,128]{2,1,0:T(8,128)}, f32[8,128]{1,0:T(8,128)S(1)}) custom-call(s32[1]{0:T(128)} %bitcast._.at_ref, f32[8,48,128]{2,1,0:T(8,128)S(1)} %all_to_all.16.recv_ref, f32[8,128]{1,0:T(8,128)S(1)} %get-tuple-element.14.rate_ref, f32[8,128]{1,0:T(8,128)S(1)} %get-tuple-element.16.arrive_ref), custom_call_target="tpu_custom_call" | custom-call | tf_op jit(solution)/shard_map/column/pallas_call | solution.py:291
  31.7 0.0 copy-start
  31.7 0.0 copy-start.1
  31.7 7.7 %all-to-all-start.2 = ((f32[8,16,128]{2,1,0:T(8,128)}), f32[8,16,128]{2,1,0:T(8,128)S(1)}, u32[]{:S(2)}, u32[]{:S(2)}) async-start(f32[8,16,128]{2,1,0:T(8,128)} %get-tuple-element.18), calls=%async_computation.2 | async-start | bytes 131072 | tf_op jit(solution)/shard_map/all_to_all | solution.py:299
  39.4 0.0 copy-done
  39.4 0.0 copy-done.1
  39.4 2.1 %post.1 = bf16[64,512]{1,0:T(8,128)(2,1)} custom-call(f32[256,128]{1,0:T(8,128)S(1)} %get-tuple-element.12.gt_ref, f32[16,64]{1,0:T(8,128)S(1)} %bitcast.18, f32[16,64]{1,0:T(8,128)S(1)} %get-tuple-element.23.weight_ref, f32[8,128]{1,0:T(8,128)S(1)} %get-tuple-element.17.state_ref), custom_call_target="tpu_custom_call" | custom-call | tf_op jit(solution)/shard_map/post/pallas_call | solution.py:303
  41.6 0.6 %all-to-all-done.2.recv_ref = f32[8,16,128]{2,1,0:T(8,128)S(1)} async-done(((f32[8,16,128]{2,1,0:T(8,128)}), f32[8,16,128]{2,1,0:T(8,128)S(1)}, u32[]{:S(2)}, u32[]{:S(2)}) %all-to-all-start.2) | async-done | bytes 65568 | tf_op jit(solution)/shard_map/all_to_all | solution.py:299
  42.1 0.7 %final.1 = (f32[16,64]{1,0:T(8,128)}, f32[16,64]{1,0:T(8,128)}) custom-call(f32[8,16,128]{2,1,0:T(8,128)S(1)} %all-to-all-done.2.recv_ref, f32[16,64]{1,0:T(8,128)S(1)} %get-tuple-element.24.one_ref, f32[16,64]{1,0:T(8,128)S(1)} %get-tuple-element.22.two_ref, f32[16,64]{1,0:T(8,128)S(1)} %get-tuple-element.21.three_ref), custom_call_target="tpu_custom_call" | custom-call | tf_op jit(solution)/shard_map/final/pallas_call | solution.py:314
  (2 shorter events, 0.1 us)
Async XLA Ops:
  31.7 7.7 %copy-start = (f32[64,16]{0,1:T(8,128)S(1)}, f32[64,16]{0,1:T(8,128)}, u32[]{:S(2)}) copy-start(f32[64,16]{0,1:T(8,128)} %param.6) | copy-start | bytes 12292
  31.7 7.7 %copy-start.1 = (f32[64,16]{0,1:T(8,128)S(1)}, f32[64,16]{0,1:T(8,128)}, u32[]{:S(2)}) copy-start(f32[64,16]{0,1:T(8,128)} %param.7) | copy-start | bytes 12292
  31.7 10.4 %all-to-all-start.2 = ((f32[8,16,128]{2,1,0:T(8,128)}), f32[8,16,128]{2,1,0:T(8,128)S(1)}, u32[]{:S(2)}, u32[]{:S(2)}) async-start(f32[8,16,128]{2,1,0:T(8,128)} %get-tuple-element.18), calls=%async_computation.2 | async-start | bytes 131072 | tf_op jit(solution)/shard_map/all_to_all | solution.py:299

commit v6 on v5

--- a/solution.py
+++ b/solution.py
@@ -22,8 +22,8 @@
 ROWS = 8
 GROUP = 8
 ROW_ORDER = [6, 5, 4, 3, 2, 1, 0, 7]
-COLUMN_ORDER = [4, 3, 2, 1, 0, 7, 6, 5]
-CHANNEL_ORDER = [5, 4, 3, 2, 1, 0, 7, 6]
+COLUMN_ORDER = [4, 5, 3, 2, 0, 1, 7, 6]
+CHANNEL_ORDER = [5, 7, 1, 3, 4, 6, 0, 2]
 GRANT = pltpu.CompilerParams(vmem_limit_bytes=8 << 20)
 
 

time: 43.2 us -> 43.1 us (level)
  no operation moved by 1% of the time
where the time goes in v6:
time: 43.1 us; the launch traced here: 42.8 us
  blocking collectives  28.5 us (66%)
  starting transfers between devices  7.43 us (17%)
  Pallas kernels  5.63 us (13%)
  between operations  0.66 us (2%)
  waiting for transfers between devices  0.52 us (1%)
    all_to_all x1, blocking collectives, body(): lax.all_to_all(message, 'context', 0, 0, axis_index_groups=rows, tiled=True)  16.8 us
    all_to_all x1, blocking collectives, body(): lax.all_to_all(message, 'context', 0, 0, axis_index_groups=columns, tiled...  11.7 us
    all_to_all x1, starting transfers between devices, body(): lax.all_to_all(message, 'channel', 0, 0, axis_index_groups=[CHANNEL_ORDER...  7.43 us
    pallas_call x1, Pallas kernels, first_call(): pl.pallas_call(pre_kernel, out_shape=(f32(ROWS, 6 * SUBLANES, LANES), f32...  2.13 us
    pallas_call x1, Pallas kernels, body(): pl.pallas_call(post_kernel, out_shape=jax.ShapeDtypeStruct((CHANNELS, CHU...  2.1 us
  transfers between devices with their start and end apart: 1, of which 1 were waited for; matrix products, arithmetic and copies ran while one was open for 0% of the time, Pallas kernels for 5%

profile of v6, /device:TPU:1, one launch (start us, length us, event | category | flops | bytes accessed | tf_op | source)
XLA Modules:
  0.0 42.8 jit_solution(7070249752736621156)
XLA Ops:
  0.6 2.1 %pre.1 = (f32[8,48,128]{2,1,0:T(8,128)S(1)}, f32[256,128]{1,0:T(8,128)S(1)}, f32[8,128]{1,0:T(8,128)S(1)}) custom-call(s32[1]{0:T(128)} %bitcast._.at_ref, bf16[64,512]{1,0:T(8,128)(2,1)} %x_hbm.1, bf16[64,512]{1,0:T(8,128)(2,1)} %g_hbm.1, f32[16,64]{1,0:T(8,128)} %bitcast.17), custom_call_target="tpu_custom_call" | custom-call | tf_op jit(solution)/shard_map/pre/pallas_call | solution.py:252
  2.8 16.8 %all_to_all.15.recv_ref = f32[8,48,128]{2,1,0:T(8,128)S(1)} all-to-all(f32[8,48,128]{2,1,0:T(8,128)S(1)} %get-tuple-element.13), channel_id=1, replica_groups={{48,40,32,24,16,8,0,56},{112,104,96,88,80,72,64,120},{176,168,160,152,1..., dimensions={0} | all-to-all | bytes 393216 | tf_op jit(solution)/shard_map/all_to_all | solution.py:281
  19.6 11.7 %all_to_all.16.recv_ref = f32[8,48,128]{2,1,0:T(8,128)S(1)} all-to-all(f32[8,48,128]{2,1,0:T(8,128)S(1)} %get-tuple-element.15), channel_id=1, replica_groups={{256,320,192,128,0,64,448,384},{264,328,200,136,8,72,456,392},{272,336,..., dimensions={0} | all-to-all | bytes 393216 | tf_op jit(solution)/shard_map/all_to_all | solution.py:290
  31.3 0.7 %column.1 = (f32[8,16,128]{2,1,0:T(8,128)}, f32[8,128]{1,0:T(8,128)S(1)}) custom-call(s32[1]{0:T(128)} %bitcast._.at_ref, f32[8,48,128]{2,1,0:T(8,128)S(1)} %all_to_all.16.recv_ref, f32[8,128]{1,0:T(8,128)S(1)} %get-tuple-element.14.rate_ref, f32[8,128]{1,0:T(8,128)S(1)} %get-tuple-element.16.arrive_ref), custom_call_target="tpu_custom_call" | custom-call | tf_op jit(solution)/shard_map/column/pallas_call | solution.py:291
  32.0 0.0 copy-start
  32.0 0.0 copy-start.1
  32.0 7.4 %all-to-all-start.2 = ((f32[8,16,128]{2,1,0:T(8,128)}), f32[8,16,128]{2,1,0:T(8,128)S(1)}, u32[]{:S(2)}, u32[]{:S(2)}) async-start(f32[8,16,128]{2,1,0:T(8,128)} %get-tuple-element.18), calls=%async_computation.2 | async-start | bytes 131072 | tf_op jit(solution)/shard_map/all_to_all | solution.py:299
  39.4 0.0 copy-done
  39.4 0.0 copy-done.1
  39.4 2.1 %post.1 = bf16[64,512]{1,0:T(8,128)(2,1)} custom-call(f32[256,128]{1,0:T(8,128)S(1)} %get-tuple-element.12.gt_ref, f32[16,64]{1,0:T(8,128)S(1)} %bitcast.18, f32[16,64]{1,0:T(8,128)S(1)} %get-tuple-element.23.weight_ref, f32[8,128]{1,0:T(8,128)S(1)} %get-tuple-element.17.state_ref), custom_call_target="tpu_custom_call" | custom-call | tf_op jit(solution)/shard_map/post/pallas_call | solution.py:303
  41.6 0.5 %all-to-all-done.2.recv_ref = f32[8,16,128]{2,1,0:T(8,128)S(1)} async-done(((f32[8,16,128]{2,1,0:T(8,128)}), f32[8,16,128]{2,1,0:T(8,128)S(1)}, u32[]{:S(2)}, u32[]{:S(2)}) %all-to-all-start.2) | async-done | bytes 65568 | tf_op jit(solution)/shard_map/all_to_all | solution.py:299
  42.1 0.7 %final.1 = (f32[16,64]{1,0:T(8,128)}, f32[16,64]{1,0:T(8,128)}) custom-call(f32[8,16,128]{2,1,0:T(8,128)S(1)} %all-to-all-done.2.recv_ref, f32[16,64]{1,0:T(8,128)S(1)} %get-tuple-element.24.one_ref, f32[16,64]{1,0:T(8,128)S(1)} %get-tuple-element.22.two_ref, f32[16,64]{1,0:T(8,128)S(1)} %get-tuple-element.21.three_ref), custom_call_target="tpu_custom_call" | custom-call | tf_op jit(solution)/shard_map/final/pallas_call | solution.py:314
  (2 shorter events, 0.1 us)
Async XLA Ops:
  32.0 7.4 %copy-start = (f32[64,16]{0,1:T(8,128)S(1)}, f32[64,16]{0,1:T(8,128)}, u32[]{:S(2)}) copy-start(f32[64,16]{0,1:T(8,128)} %param.6) | copy-start | bytes 12292
  32.0 7.4 %copy-start.1 = (f32[64,16]{0,1:T(8,128)S(1)}, f32[64,16]{0,1:T(8,128)}, u32[]{:S(2)}) copy-start(f32[64,16]{0,1:T(8,128)} %param.7) | copy-start | bytes 12292
  32.0 10.1 %all-to-all-start.2 = ((f32[8,16,128]{2,1,0:T(8,128)}), f32[8,16,128]{2,1,0:T(8,128)S(1)}, u32[]{:S(2)}, u32[]{:S(2)}) async-start(f32[8,16,128]{2,1,0:T(8,128)} %get-tuple-element.18), calls=%async_computation.2 | async-start | bytes 131072 | tf_op jit(solution)/shard_map/all_to_all | solution.py:299

commit v7 on v6

--- a/solution.py
+++ b/solution.py
@@ -15,10 +15,10 @@
 STEP = 32
 HALF = SUBLANES * STEP
 CHUNK = 2 * HALF
-BLOCKS = 4
+BLOCKS = 8
 BLOCK = HALF // BLOCKS
 UNROLL = 16
-POSTU = 8
+POSTU = 32
 ROWS = 8
 GROUP = 8
 ROW_ORDER = [6, 5, 4, 3, 2, 1, 0, 7]
@@ -46,7 +46,7 @@
     return stacked.astype(jnp.float32).T
 
 
-def pre_kernel(_, x_hbm, g_hbm, rate_hbm, msg_ref, gt_ref, packed_ref, x_ref, g_ref, rate_ref, xt_ref, rows_ref, sems):
+def pre_kernel(_, x_hbm, g_hbm, rate_hbm, msg_ref, gt_ref, packed_ref, entry_ref, x_ref, g_ref, rate_ref, xt_ref, rows_ref, sems):
     copies = [
         pltpu.make_async_copy(source, target, sems.at[i])
         for i, (source, target) in enumerate(((rate_hbm, rate_ref), (g_hbm, g_ref), (x_hbm, x_ref)))
@@ -88,8 +88,10 @@
     reach = jnp.exp(-float(BLOCK) * rate)
     coming, coming_slope = total[-1], slope[-1]
     behind, behind_lean = state[0], lean[0]
+    enter = [zero] * BLOCKS
     for b in range(1, BLOCKS):
         back = BLOCKS - 1 - b
+        enter[back] = coming
         value = value + state[back] * coming
         tilt = tilt + lean[back] * coming + state[back] * coming_slope
         coming_slope = slope[back] + reach * (coming_slope + float(BLOCK) * coming)
@@ -99,6 +101,10 @@
     low = low_half(zero.shape)
     turn = lambda v: pltpu.roll(v, CHANNELS, 1)
     late, late_slope = turn(coming), turn(coming_slope)
+    passing = jnp.where(low, late, 0.0)
+    for b in reversed(range(BLOCKS)):
+        entry_ref[pl.ds(b * POLES, POLES), :] = enter[b] + passing
+        passing = reach * passing
     value = value + jnp.where(low, behind * late, 0.0)
     tilt = tilt + jnp.where(low, behind_lean * late + behind * late_slope, 0.0)
     jump = jnp.exp(-float(HALF) * rate)
@@ -166,7 +172,12 @@
     state_ref[...] = arrive_ref[...] + jnp.exp(-after * rate) * pick(lax.div(at_ref[0], ROWS), sums[6])
 
 
-def post_kernel(gt_ref, rate_ref, weight_ref, state_ref, out_ref, yt_ref):
+def last_kernel(gt_ref, entry_ref, rate_ref, weight_ref, state_ref, recv_ref, one_ref, two_ref, three_ref, out_ref, res_ref, log_ref, yt_ref):
+    final_kernel(recv_ref, one_ref, two_ref, three_ref, res_ref, log_ref)
+    post_kernel(gt_ref, entry_ref, rate_ref, weight_ref, state_ref, out_ref, yt_ref)
+
+
+def post_kernel(gt_ref, entry_ref, rate_ref, weight_ref, state_ref, out_ref, yt_ref):
     full = (SUBLANES, LANES)
     low = low_half(full)
     low_row = low_half((1, LANES))
@@ -176,33 +187,17 @@
     rates = double(rate_ref[...])
     weights = double(weight_ref[...])
     decays = jnp.exp(-rates)
-    spans = jnp.exp(-float(STEP) * rates)
     wide = lambda rows, k: jnp.broadcast_to(rows[k : k + 1], full)
     for first in range(0, POLES, 8):
         poles = range(first, first + 8)
         decay = [wide(decays, k) for k in poles]
 
-        def ends(at, total):
-            g = gt_ref[pl.ds(STEP - 1 - at, SUBLANES, stride=STEP), :]
-            return [decay[i] * total[i] + g for i in range(8)]
-
-        blank = [jnp.zeros(full, jnp.float32)] * 8
-        local = lax.fori_loop(0, STEP, ends, blank, unroll=POSTU)
         entry = []
-        for i, k in enumerate(poles):
-            total = local[i]
-            far = wide(spans, k)
-            for shift in (1, 2, 4):
-                moved = pltpu.roll(total, SUBLANES - shift, 0)
-                total = total + jnp.where(block < SUBLANES - shift, far * moved, 0.0)
-                far = far * far
-            inside = jnp.where(block < SUBLANES - 1, pltpu.roll(total, SUBLANES - 1, 0), 0.0)
-            late = jnp.where(low, pltpu.roll(jnp.broadcast_to(total[0:1], full), CHANNELS, 1), 0.0)
+        for k in poles:
             row = state_ref[pl.ds(k // 2, 1), :]
             other = pltpu.roll(row, CHANNELS, 1)
             both = jnp.where(low_row, row, other) if k % 2 == 0 else jnp.where(low_row, other, row)
-            rate = rates[k : k + 1]
-            entry.append(inside + jnp.exp(-after * rate) * late + jnp.exp(-away * rate) * both)
+            entry.append(entry_ref[pl.ds(k, SUBLANES, stride=POLES), :] + jnp.exp(-away * rates[k : k + 1]) * both)
         weight = [wide(weights, k) for k in poles]
 
         def outputs(at, total):
@@ -251,9 +246,9 @@
 def first_call(at, x, g, rate, name="pre"):
     return pl.pallas_call(
         pre_kernel,
-        out_shape=(f32(ROWS, 6 * SUBLANES, LANES), f32(HALF, LANES), f32(SUBLANES, LANES)),
+        out_shape=(f32(ROWS, 6 * SUBLANES, LANES), f32(HALF, LANES), f32(SUBLANES, LANES), f32(LANES, LANES)),
         in_specs=[pl.BlockSpec(memory_space=pltpu.SMEM)] + [pl.BlockSpec(memory_space=pltpu.HBM)] * 3,
-        out_specs=tuple(vmem(3)),
+        out_specs=tuple(vmem(4)),
         scratch_shapes=[
             pltpu.VMEM((CHANNELS, CHUNK), jnp.bfloat16),
             pltpu.VMEM((CHANNELS, CHUNK), jnp.bfloat16),
@@ -275,7 +270,7 @@
     columns = [[y * ROWS + z for y in COLUMN_ORDER] for z in range(ROWS)]
     smem = [pl.BlockSpec(memory_space=pltpu.SMEM)]
 
-    message, turned, packed = first_call(
+    message, turned, packed, entry = first_call(
         at, *(pltpu.with_memory_space_constraint(v, pltpu.HBM) for v in (inputs, grad_out, rate))
     )
     received = lax.all_to_all(message, "context", 0, 0, axis_index_groups=rows, tiled=True)
@@ -298,27 +293,20 @@
     )(at, received, packed, arrived)
     received = lax.all_to_all(message, "channel", 0, 0, axis_index_groups=[CHANNEL_ORDER], tiled=True)
 
+    received, rate, residue = lax.optimization_barrier((received, rate, residue))
     gain = jnp.sqrt(-jnp.expm1(-2.0 * rate))
     decay = jnp.exp(-rate)
-    grad_in = pl.pallas_call(
-        post_kernel,
-        out_shape=jax.ShapeDtypeStruct((CHANNELS, CHUNK), jnp.bfloat16),
-        in_specs=vmem(4),
-        out_specs=vmem(1)[0],
+    norm = 1.0 / math.sqrt(CHUNK * ROWS * ROWS * GROUP)
+    scaled = residue * rate * norm
+    grad_in, res_grad, log_grad = pl.pallas_call(
+        last_kernel,
+        out_shape=(jax.ShapeDtypeStruct((CHANNELS, CHUNK), jnp.bfloat16), f32(POLES, CHANNELS), f32(POLES, CHANNELS)),
+        in_specs=vmem(9),
+        out_specs=tuple(vmem(3)),
         scratch_shapes=[scratch(HALF, LANES)],
         compiler_params=GRANT,
-        name="post",
-    )(turned, rate, residue * gain, state)
-    norm = 1.0 / math.sqrt(CHUNK * ROWS * ROWS * GROUP)
-    scaled = residue * rate * norm
-    res_grad, log_grad = pl.pallas_call(
-        final_kernel,
-        out_shape=(f32(POLES, CHANNELS), f32(POLES, CHANNELS)),
-        in_specs=vmem(4),
-        out_specs=tuple(vmem(2)),
-        compiler_params=GRANT,
-        name="final",
-    )(received, gain * norm, scaled * (decay * decay / gain), scaled * gain)
+        name="last",
+    )(turned, entry, rate, residue * gain, state, received, gain * norm, scaled * (decay * decay / gain), scaled * gain)
     return (grad_in, res_grad.T, log_grad.T)
 
 

time: 43.1 us -> 42.6 us (0.988)
  blocking collectives: 28.5 us -> 37.9 us
  starting transfers between devices: 7.43 us -> 0 us
  Pallas kernels: 5.63 us -> 3.69 us
  waiting for transfers between devices: 0.52 us -> 0 us
    all_to_all x0 -> x1, blocking collectives: none -> 9.42 us  [body(): lax.all_to_all(message, 'channel', 0, 0, axis_index_groups=[CHANNEL_ORDER...]
    all_to_all x1 -> x0, starting transfers between devices: 7.43 us -> none  [body(): lax.all_to_all(message, 'channel', 0, 0, axis_index_groups=[CHANNEL_ORDER...]
    pallas_call x2 -> x1, Pallas kernels: 2.8 us -> 1.4 us  [body(): pl.pallas_call(last_kernel, out_shape=(jax.ShapeDtypeStruct((CHANNELS, CH...]
    pallas_call x1, Pallas kernels: 0.67 us -> 0.03 us  [body(): pl.pallas_call(column_kernel, out_shape=(f32(GROUP, 2 * SUBLANES, LANES),...]
    all_to_all x1 -> x0, waiting for transfers between devices: 0.52 us -> none  [body(): lax.all_to_all(message, 'channel', 0, 0, axis_index_groups=[CHANNEL_ORDER...]
  transfers between devices with their start and end apart: 1 -> 0, of which waited for: 1 -> 0; matrix products, arithmetic and copies ran while one was open for 0% -> 0% of each run, Pallas kernels for 5% -> 0%
where the time goes in v7:
time: 42.6 us; the launch traced here: 42.3 us
  blocking collectives  37.9 us (89%)
  Pallas kernels  3.69 us (9%)
  between operations  0.68 us (2%)
    all_to_all x1, blocking collectives, body(): lax.all_to_all(message, 'context', 0, 0, axis_index_groups=rows, tiled=True)  16.8 us
    all_to_all x1, blocking collectives, body(): lax.all_to_all(message, 'context', 0, 0, axis_index_groups=columns, tiled...  11.7 us
    all_to_all x1, blocking collectives, body(): lax.all_to_all(message, 'channel', 0, 0, axis_index_groups=[CHANNEL_ORDER...  9.42 us
    pallas_call x1, Pallas kernels, first_call(): pl.pallas_call(pre_kernel, out_shape=(f32(ROWS, 6 * SUBLANES, LANES), f32...  2.21 us
    pallas_call x1, Pallas kernels, body(): pl.pallas_call(last_kernel, out_shape=(jax.ShapeDtypeStruct((CHANNELS, CH...  1.4 us

profile of v7, /device:TPU:1, one launch (start us, length us, event | category | flops | bytes accessed | tf_op | source)
XLA Modules:
  0.0 42.3 jit_solution(736029209596749210)
XLA Ops:
  0.6 2.2 %pre.1 = (f32[8,48,128]{2,1,0:T(8,128)S(1)}, f32[256,128]{1,0:T(8,128)S(1)}, f32[8,128]{1,0:T(8,128)S(1)}, f32[128,128]{1,0:T(8,128)S(1)}) custom-call(s32[1]{0:T(128)} %bitcast._.at_ref, bf16[64,512]{1,0:T(8,128)(2,1)} %x_hbm.1, bf16[64,512]{1,0:T(8,128)(2,1)} %g_hbm.1, f32[16,64]{1,0:T(8,128)} %bitcast.5), custom_call_target="tpu_custom_call" | custom-call | tf_op jit(solution)/shard_map/pre/pallas_call | solution.py:247
  2.9 16.8 %all_to_all.15.recv_ref = f32[8,48,128]{2,1,0:T(8,128)S(1)} all-to-all(f32[8,48,128]{2,1,0:T(8,128)S(1)} %get-tuple-element.19), channel_id=1, replica_groups={{48,40,32,24,16,8,0,56},{112,104,96,88,80,72,64,120},{176,168,160,152,1..., dimensions={0} | all-to-all | bytes 393216 | tf_op jit(solution)/shard_map/all_to_all | solution.py:276
  19.6 11.7 %all_to_all.16.recv_ref = f32[8,48,128]{2,1,0:T(8,128)S(1)} all-to-all(f32[8,48,128]{2,1,0:T(8,128)S(1)} %get-tuple-element.21), channel_id=1, replica_groups={{256,320,192,128,0,64,448,384},{264,328,200,136,8,72,456,392},{272,336,..., dimensions={0} | all-to-all | bytes 393216 | tf_op jit(solution)/shard_map/all_to_all | solution.py:285
  31.4 0.0 copy-start
  31.4 0.0 copy-start.1
  31.5 9.4 %all_to_all.17.recv_ref = f32[8,16,128]{2,1,0:T(8,128)S(1)} all-to-all(f32[8,16,128]{2,1,0:T(8,128)S(1)} %get-tuple-element.23), channel_id=1, replica_groups={{5,7,1,3,4,6,0,2},{13,15,9,11,12,14,8,10},{21,23,17,19,20,22,16,18},{29..., dimensions={0} | all-to-all | bytes 131072 | tf_op jit(solution)/shard_map/all_to_all | solution.py:294
  40.9 0.0 copy-done
  40.9 0.0 copy-done.1
  40.9 1.4 %last.1 = (bf16[64,512]{1,0:T(8,128)(2,1)}, f32[16,64]{1,0:T(8,128)}, f32[16,64]{1,0:T(8,128)}) custom-call(f32[256,128]{1,0:T(8,128)S(1)} %get-tuple-element.17.gt_ref, f32[128,128]{1,0:T(8,128)S(1)} %get-tuple-element.18.entry_ref, f32[16,64]{1,0:T(8,128)S(1)} %bitcast.7, f32[16,64]{1,0:T(8,128)S(1)} %get-tuple-element.33.weight_ref, ...), custom_call_target="tpu_custom_call" | custom-call | tf_op jit(solution)/shard_map/last/pallas_call | solution.py:301
  (3 shorter events, 0.1 us)
Async XLA Ops:
  31.4 9.4 %copy-start = (f32[64,16]{0,1:T(8,128)S(1)}, f32[64,16]{0,1:T(8,128)}, u32[]{:S(2)}) copy-start(f32[64,16]{0,1:T(8,128)} %param.6) | copy-start | bytes 12292
  31.4 9.4 %copy-start.1 = (f32[64,16]{0,1:T(8,128)S(1)}, f32[64,16]{0,1:T(8,128)}, u32[]{:S(2)}) copy-start(f32[64,16]{0,1:T(8,128)} %param.7) | copy-start | bytes 12292

commit v8 on v7

--- a/solution.py
+++ b/solution.py
@@ -19,6 +19,7 @@
 BLOCK = HALF // BLOCKS
 UNROLL = 16
 POSTU = 32
+WIDTH = 16
 ROWS = 8
 GROUP = 8
 ROW_ORDER = [6, 5, 4, 3, 2, 1, 0, 7]
@@ -188,8 +189,8 @@
     weights = double(weight_ref[...])
     decays = jnp.exp(-rates)
     wide = lambda rows, k: jnp.broadcast_to(rows[k : k + 1], full)
-    for first in range(0, POLES, 8):
-        poles = range(first, first + 8)
+    for first in range(0, POLES, WIDTH):
+        poles = range(first, first + WIDTH)
         decay = [wide(decays, k) for k in poles]
 
         entry = []
@@ -203,8 +204,8 @@
         def outputs(at, total):
             rows = pl.ds(STEP - 1 - at, SUBLANES, stride=STEP)
             g = gt_ref[rows, :]
-            total = [decay[i] * total[i] + g for i in range(8)]
-            terms = [weight[i] * total[i] for i in range(8)]
+            total = [decay[i] * total[i] + g for i in range(WIDTH)]
+            terms = [weight[i] * total[i] for i in range(WIDTH)]
             while len(terms) > 1:
                 terms = [terms[i] + terms[i + 1] for i in range(0, len(terms), 2)]
             yt_ref[rows, :] = terms[0] if first == 0 else yt_ref[rows, :] + terms[0]

time: 42.6 us -> 42.5 us (level)
  no operation moved by 1% of the time
where the time goes in v8:
time: 42.5 us; the launch traced here: 42.2 us
  blocking collectives  37.9 us (89%)
  Pallas kernels  3.56 us (8%)
  between operations  0.68 us (2%)
    all_to_all x1, blocking collectives, body(): lax.all_to_all(message, 'context', 0, 0, axis_index_groups=rows, tiled=True)  16.8 us
    all_to_all x1, blocking collectives, body(): lax.all_to_all(message, 'context', 0, 0, axis_index_groups=columns, tiled...  11.7 us
    all_to_all x1, blocking collectives, body(): lax.all_to_all(message, 'channel', 0, 0, axis_index_groups=[CHANNEL_ORDER...  9.42 us
    pallas_call x1, Pallas kernels, first_call(): pl.pallas_call(pre_kernel, out_shape=(f32(ROWS, 6 * SUBLANES, LANES), f32...  2.21 us
    pallas_call x1, Pallas kernels, body(): pl.pallas_call(last_kernel, out_shape=(jax.ShapeDtypeStruct((CHANNELS, CH...  1.28 us

profile of v8, /device:TPU:1, one launch (start us, length us, event | category | flops | bytes accessed | tf_op | source)
XLA Modules:
  0.0 42.2 jit_solution(12387934177874226735)
XLA Ops:
  0.6 2.2 %pre.1 = (f32[8,48,128]{2,1,0:T(8,128)S(1)}, f32[256,128]{1,0:T(8,128)S(1)}, f32[8,128]{1,0:T(8,128)S(1)}, f32[128,128]{1,0:T(8,128)S(1)}) custom-call(s32[1]{0:T(128)} %bitcast._.at_ref, bf16[64,512]{1,0:T(8,128)(2,1)} %x_hbm.1, bf16[64,512]{1,0:T(8,128)(2,1)} %g_hbm.1, f32[16,64]{1,0:T(8,128)} %bitcast.5), custom_call_target="tpu_custom_call" | custom-call | tf_op jit(solution)/shard_map/pre/pallas_call | solution.py:248
  2.9 16.8 %all_to_all.15.recv_ref = f32[8,48,128]{2,1,0:T(8,128)S(1)} all-to-all(f32[8,48,128]{2,1,0:T(8,128)S(1)} %get-tuple-element.19), channel_id=1, replica_groups={{48,40,32,24,16,8,0,56},{112,104,96,88,80,72,64,120},{176,168,160,152,1..., dimensions={0} | all-to-all | bytes 393216 | tf_op jit(solution)/shard_map/all_to_all | solution.py:277
  19.6 11.7 %all_to_all.16.recv_ref = f32[8,48,128]{2,1,0:T(8,128)S(1)} all-to-all(f32[8,48,128]{2,1,0:T(8,128)S(1)} %get-tuple-element.21), channel_id=1, replica_groups={{256,320,192,128,0,64,448,384},{264,328,200,136,8,72,456,392},{272,336,..., dimensions={0} | all-to-all | bytes 393216 | tf_op jit(solution)/shard_map/all_to_all | solution.py:286
  31.4 0.0 copy-start
  31.4 0.0 copy-start.1
  31.5 9.4 %all_to_all.17.recv_ref = f32[8,16,128]{2,1,0:T(8,128)S(1)} all-to-all(f32[8,16,128]{2,1,0:T(8,128)S(1)} %get-tuple-element.23), channel_id=1, replica_groups={{5,7,1,3,4,6,0,2},{13,15,9,11,12,14,8,10},{21,23,17,19,20,22,16,18},{29..., dimensions={0} | all-to-all | bytes 131072 | tf_op jit(solution)/shard_map/all_to_all | solution.py:295
  40.9 0.0 copy-done
  40.9 0.0 copy-done.1
  40.9 1.3 %last.1 = (bf16[64,512]{1,0:T(8,128)(2,1)}, f32[16,64]{1,0:T(8,128)}, f32[16,64]{1,0:T(8,128)}) custom-call(f32[256,128]{1,0:T(8,128)S(1)} %get-tuple-element.17.gt_ref, f32[128,128]{1,0:T(8,128)S(1)} %get-tuple-element.18.entry_ref, f32[16,64]{1,0:T(8,128)S(1)} %bitcast.7, f32[16,64]{1,0:T(8,128)S(1)} %get-tuple-element.33.weight_ref, ...), custom_call_target="tpu_custom_call" | custom-call | tf_op jit(solution)/shard_map/last/pallas_call | solution.py:302
  (3 shorter events, 0.1 us)
Async XLA Ops:
  31.4 9.4 %copy-start = (f32[64,16]{0,1:T(8,128)S(1)}, f32[64,16]{0,1:T(8,128)}, u32[]{:S(2)}) copy-start(f32[64,16]{0,1:T(8,128)} %param.6) | copy-start | bytes 12292
  31.4 9.4 %copy-start.1 = (f32[64,16]{0,1:T(8,128)S(1)}, f32[64,16]{0,1:T(8,128)}, u32[]{:S(2)}) copy-start(f32[64,16]{0,1:T(8,128)} %param.7) | copy-start | bytes 12292

commit v9 on v8

--- a/solution.py
+++ b/solution.py
@@ -24,7 +24,7 @@
 GROUP = 8
 ROW_ORDER = [6, 5, 4, 3, 2, 1, 0, 7]
 COLUMN_ORDER = [4, 5, 3, 2, 0, 1, 7, 6]
-CHANNEL_ORDER = [5, 7, 1, 3, 4, 6, 0, 2]
+CHANNEL_ORDER = [5, 7, 1, 3, 0, 2, 4, 6]
 GRANT = pltpu.CompilerParams(vmem_limit_bytes=8 << 20)
 
 

time: 42.5 us -> 42.5 us (level)
  no operation moved by 1% of the time
where the time goes in v9:
time: 42.5 us; the launch traced here: 42.2 us
  blocking collectives  37.9 us (89%)
  Pallas kernels  3.56 us (8%)
  between operations  0.68 us (2%)
    all_to_all x1, blocking collectives, body(): lax.all_to_all(message, 'context', 0, 0, axis_index_groups=rows, tiled=True)  16.8 us
    all_to_all x1, blocking collectives, body(): lax.all_to_all(message, 'context', 0, 0, axis_index_groups=columns, tiled...  11.7 us
    all_to_all x1, blocking collectives, body(): lax.all_to_all(message, 'channel', 0, 0, axis_index_groups=[CHANNEL_ORDER...  9.41 us
    pallas_call x1, Pallas kernels, first_call(): pl.pallas_call(pre_kernel, out_shape=(f32(ROWS, 6 * SUBLANES, LANES), f32...  2.21 us
    pallas_call x1, Pallas kernels, body(): pl.pallas_call(last_kernel, out_shape=(jax.ShapeDtypeStruct((CHANNELS, CH...  1.28 us

profile of v9, /device:TPU:1, one launch (start us, length us, event | category | flops | bytes accessed | tf_op | source)
XLA Modules:
  0.0 42.2 jit_solution(6115285439950609540)
XLA Ops:
  0.6 2.2 %pre.1 = (f32[8,48,128]{2,1,0:T(8,128)S(1)}, f32[256,128]{1,0:T(8,128)S(1)}, f32[8,128]{1,0:T(8,128)S(1)}, f32[128,128]{1,0:T(8,128)S(1)}) custom-call(s32[1]{0:T(128)} %bitcast._.at_ref, bf16[64,512]{1,0:T(8,128)(2,1)} %x_hbm.1, bf16[64,512]{1,0:T(8,128)(2,1)} %g_hbm.1, f32[16,64]{1,0:T(8,128)} %bitcast.5), custom_call_target="tpu_custom_call" | custom-call | tf_op jit(solution)/shard_map/pre/pallas_call | solution.py:248
  2.9 16.8 %all_to_all.15.recv_ref = f32[8,48,128]{2,1,0:T(8,128)S(1)} all-to-all(f32[8,48,128]{2,1,0:T(8,128)S(1)} %get-tuple-element.19), channel_id=1, replica_groups={{48,40,32,24,16,8,0,56},{112,104,96,88,80,72,64,120},{176,168,160,152,1..., dimensions={0} | all-to-all | bytes 393216 | tf_op jit(solution)/shard_map/all_to_all | solution.py:277
  19.6 11.7 %all_to_all.16.recv_ref = f32[8,48,128]{2,1,0:T(8,128)S(1)} all-to-all(f32[8,48,128]{2,1,0:T(8,128)S(1)} %get-tuple-element.21), channel_id=1, replica_groups={{256,320,192,128,0,64,448,384},{264,328,200,136,8,72,456,392},{272,336,..., dimensions={0} | all-to-all | bytes 393216 | tf_op jit(solution)/shard_map/all_to_all | solution.py:286
  31.4 0.0 copy-start
  31.4 0.0 copy-start.1
  31.5 9.4 %all_to_all.17.recv_ref = f32[8,16,128]{2,1,0:T(8,128)S(1)} all-to-all(f32[8,16,128]{2,1,0:T(8,128)S(1)} %get-tuple-element.23), channel_id=1, replica_groups={{5,7,1,3,0,2,4,6},{13,15,9,11,8,10,12,14},{21,23,17,19,16,18,20,22},{29..., dimensions={0} | all-to-all | bytes 131072 | tf_op jit(solution)/shard_map/all_to_all | solution.py:295
  40.9 0.0 copy-done
  40.9 0.0 copy-done.1
  40.9 1.3 %last.1 = (bf16[64,512]{1,0:T(8,128)(2,1)}, f32[16,64]{1,0:T(8,128)}, f32[16,64]{1,0:T(8,128)}) custom-call(f32[256,128]{1,0:T(8,128)S(1)} %get-tuple-element.17.gt_ref, f32[128,128]{1,0:T(8,128)S(1)} %get-tuple-element.18.entry_ref, f32[16,64]{1,0:T(8,128)S(1)} %bitcast.7, f32[16,64]{1,0:T(8,128)S(1)} %get-tuple-element.33.weight_ref, ...), custom_call_target="tpu_custom_call" | custom-call | tf_op jit(solution)/shard_map/last/pallas_call | solution.py:302
  (3 shorter events, 0.1 us)
Async XLA Ops:
  31.4 9.4 %copy-start = (f32[64,16]{0,1:T(8,128)S(1)}, f32[64,16]{0,1:T(8,128)}, u32[]{:S(2)}) copy-start(f32[64,16]{0,1:T(8,128)} %param.6) | copy-start | bytes 12292
  31.4 9.4 %copy-start.1 = (f32[64,16]{0,1:T(8,128)S(1)}, f32[64,16]{0,1:T(8,128)}, u32[]{:S(2)}) copy-start(f32[64,16]{0,1:T(8,128)} %param.7) | copy-start | bytes 12292
